TPU v7x, 256 devices: a whole 4x4x8 slice. The times are simulated.
256 devices in a mesh: dp: 8 (over z), fsdp: 16 (over x, y), tensor: 2 (over core).
Axes of the slice: x: 4, y: 4, z: 8, core: 2. Of those that a mesh axis runs over, the one named last changes fastest.
Arguments:
- tokens: bfloat16 [32768, 2048], P('fsdp'), may hold values from -6 to 6
- segment_ids: int32 [32768], P('fsdp'), may hold values from 0 to 127, never falling along the last dimension, each value on 1 to 512 neighbouring positions
- row_order: int32 [32768], P('fsdp'), may hold values from 0 to 2047, as said below
- row_counts: int32 [16], replicated, may hold values from 0 to 1280, as said below
- first_gain: float32 [2048], replicated, may hold values from 0.25 to 1.75
- second_gain: float32 [2048], replicated, may hold values from 0.25 to 1.75
- query_weight: bfloat16 [2048, 2048], P('fsdp', ('dp', 'tensor')), may hold values from -0.110485435 to 0.110485435
- key_weight: bfloat16 [2048, 2048], P('fsdp', ('dp', 'tensor')), may hold values from -4.4636116 to 4.4636116
- value_weight: bfloat16 [2048, 2048], P('fsdp', ('dp', 'tensor')), may hold values from -0.125 to 0.125
- output_weight: bfloat16 [2048, 2048], P(('dp', 'tensor'), 'fsdp'), may hold values from -0.125 to 0.125
- gate_weight: bfloat16 [2048, 8192], P('fsdp', ('dp', 'tensor')), may hold values from -0.125 to 0.125
- up_weight: bfloat16 [2048, 8192], P('fsdp', ('dp', 'tensor')), may hold values from -0.125 to 0.125
- down_weight: bfloat16 [8192, 2048], P(('dp', 'tensor'), 'fsdp'), may hold values from -0.0625 to 0.0625
Outputs:
- recursed: bfloat16 [32768, 2048], P('fsdp', ('dp', 'tensor'))
Inputs may be any that keep to these rules, and one draw needn't show every extreme that they name: `row_counts`: each entry is a multiple of 128, the entries sum to 16384, and the largest entry is exactly 1280. `row_order`: each shard's block of 2048 entries is a permutation of 0 to 2047.
All inputs are finite; a program needn't handle non-finite values.
Results may differ from a plain program's by a relative error of at most 0.015.
Values may be sent and summed in bfloat16 or wider, within the bound.
A program may use at most 128 MiB of HBM per device.

v0:
```python
import math

import jax
import jax.numpy as jnp
from jax import lax
from jax.sharding import PartitionSpec as P

TILE = 128


def rms_scale(row_data, gain_row):
    floats = row_data.astype(jnp.float32)
    inverse = lax.rsqrt(jnp.mean(floats * floats, axis=-1, keepdims=True) + 1e-05)
    return (floats * inverse * gain_row).astype(jnp.bfloat16)


def block_attention(queries, key_rows, value_rows, segments):
    row_total = queries.shape[0]
    block_len = math.gcd(row_total, 512)
    score_scale = 1.0 / math.sqrt(queries.shape[1])
    positions = jnp.arange(row_total, dtype=jnp.int32)

    def one_block(block_id):
        offset = block_id * block_len
        block_rows = lax.dynamic_slice_in_dim(queries, offset, block_len, 0)
        block_segs = lax.dynamic_slice_in_dim(segments, offset, block_len, 0)
        block_pos = offset + jnp.arange(block_len, dtype=jnp.int32)
        scores = (
            lax.dot_general(
                block_rows, key_rows, (((1,), (1,)), ((), ())), preferred_element_type=jnp.float32
            )
            * score_scale
        )
        allowed = (block_segs[:, None] == segments[None, :]) & (
            positions[None, :] <= block_pos[:, None]
        )
        scores = jnp.where(allowed, scores, -1e30)
        peak = jnp.max(scores, axis=-1, keepdims=True)
        expo = jnp.exp(scores - peak)
        probs = (expo / jnp.sum(expo, axis=-1, keepdims=True)).astype(jnp.bfloat16)
        return jnp.dot(probs, value_rows, preferred_element_type=jnp.float32).astype(jnp.bfloat16)

    outputs = lax.map(one_block, jnp.arange(row_total // block_len, dtype=jnp.int32))
    return outputs.reshape(row_total, queries.shape[1])


def feed_forward(ordered_cols, second_gain, gate_weight, up_weight, down_weight):
    full_rows = lax.all_gather(ordered_cols, ("dp", "tensor"), axis=1, tiled=True)
    normed = rms_scale(full_rows, second_gain)
    gate = jnp.dot(
        normed,
        lax.all_gather(gate_weight, "fsdp", axis=0, tiled=True),
        preferred_element_type=jnp.float32,
    )
    upward = jnp.dot(
        normed,
        lax.all_gather(up_weight, "fsdp", axis=0, tiled=True),
        preferred_element_type=jnp.float32,
    )
    hidden = (jax.nn.silu(gate) * upward).astype(jnp.bfloat16)
    terms = jnp.dot(
        hidden,
        lax.all_gather(down_weight, "fsdp", axis=1, tiled=True),
        preferred_element_type=jnp.float32,
    )
    return lax.psum_scatter(
        terms.astype(jnp.bfloat16), ("dp", "tensor"), scatter_dimension=1, tiled=True
    ).astype(jnp.float32)


def body(
    tokens,
    segment_ids,
    row_order,
    row_counts,
    first_gain,
    second_gain,
    query_weight,
    key_weight,
    value_weight,
    output_weight,
    gate_weight,
    up_weight,
    down_weight,
):
    normed = rms_scale(tokens, first_gain)
    weight_pieces = (
        lax.all_gather(query_weight, "fsdp", axis=0, tiled=True),
        lax.all_gather(key_weight, "fsdp", axis=0, tiled=True),
        lax.all_gather(value_weight, "fsdp", axis=0, tiled=True),
    )
    queries, key_rows, value_rows = tuple(
        (
            jnp.dot(normed, weight_piece, preferred_element_type=jnp.float32)
            for weight_piece in weight_pieces
        )
    )
    attended = block_attention(
        queries.astype(jnp.bfloat16),
        key_rows.astype(jnp.bfloat16),
        value_rows.astype(jnp.bfloat16),
        segment_ids,
    )
    head_terms = jnp.dot(
        attended,
        lax.all_gather(output_weight, "fsdp", axis=1, tiled=True),
        preferred_element_type=jnp.float32,
    )
    head_sum = lax.psum_scatter(
        head_terms.astype(jnp.bfloat16), ("dp", "tensor"), scatter_dimension=1, tiled=True
    ).astype(jnp.float32)
    share_cols = head_sum.shape[1]
    member = lax.axis_index(("dp", "tensor"))
    own_cols = lax.dynamic_slice_in_dim(tokens, member * share_cols, share_cols, 1)
    carried = (own_cols.astype(jnp.float32) + head_sum).astype(jnp.bfloat16)
    ordered = jnp.take(carried, row_order, axis=0)
    row_total = tokens.shape[0]
    live_count = lax.dynamic_index_in_dim(row_counts, lax.axis_index("fsdp"), 0, keepdims=False)
    is_live = jnp.arange(row_total, dtype=jnp.int32) < live_count
    own_tiles = row_total // TILE
    cap_rows = (own_tiles // 2 + own_tiles // 8) * TILE
    leading = ordered[:cap_rows]
    summed = feed_forward(leading, second_gain, gate_weight, up_weight, down_weight)
    finished = (leading.astype(jnp.float32) + summed).astype(jnp.bfloat16)
    updated = jnp.concatenate([finished, ordered[cap_rows:]], axis=0)
    token_rows = jnp.take(own_cols, row_order, axis=0)
    mixed = jnp.where(is_live[:, None], updated, token_rows)
    return own_cols.at[row_order].set(mixed)


def solution(mesh):
    in_specs = (
        P("fsdp", None),
        P("fsdp"),
        P("fsdp"),
        P(),
        P(),
        P(),
        P("fsdp", ("dp", "tensor")),
        P("fsdp", ("dp", "tensor")),
        P("fsdp", ("dp", "tensor")),
        P(("dp", "tensor"), "fsdp"),
        P("fsdp", ("dp", "tensor")),
        P("fsdp", ("dp", "tensor")),
        P(("dp", "tensor"), "fsdp"),
    )
    out_specs = P("fsdp", ("dp", "tensor"))
    return jax.shard_map(body, mesh=mesh, in_specs=in_specs, out_specs=out_specs, check_vma=False)
```

profile of v0, /device:TPU:1, one launch (start us, length us, event | category | flops | bytes accessed | tf_op | source)
XLA Modules:
  0.0 563.8 jit_solution(6179705660828530488)
XLA Ops:
  6.5 5.1 fusion.10
  11.7 20.0 %all_gather.26 = bf16[2048,128]{1,0:T(8,128)(2,1)S(1)} all-gather(bf16[128,128]{1,0:T(8,128)(2,1)S(1)} %copy-done.1), channel_id=1, replica_groups=mesh['dp'=8,'fsdp'=16,'tensor'=2] {'fsdp'}, dimensions={0}, use_global_device_ids=true | all-gather | bytes 557056 | tf_op jit(solution)/shard_map/all_gather | solution.py:90
  31.6 17.5 %all_gather.25 = bf16[2048,128]{1,0:T(8,128)(2,1)S(1)} all-gather(bf16[128,128]{1,0:T(8,128)(2,1)S(1)} %copy-done.2), channel_id=1, replica_groups=mesh['dp'=8,'fsdp'=16,'tensor'=2] {'fsdp'}, dimensions={0}, use_global_device_ids=true | all-gather | bytes 557056 | tf_op jit(solution)/shard_map/all_gather | solution.py:89
  49.1 8.6 %fusion.12 = bf16[2048,2048]{1,0:T(8,128)(2,1)} fusion(bf16[2048,2048]{1,0:T(8,128)(2,1)} %param.17, f32[2048]{0:T(1024)S(1)} %copy-done.7, f32[2048]{0:T(1024)S(1)} %add_rsqrt_fusion.1), kind=kLoop, calls=%fused_computation.21 | loop fusion | flops 16777216 | bytes 16793600 | tf_op jit(solution)/shard_map/convert_element_type | solution.py:14
  57.7 5.9 %convolution_convert_fusion.2 = bf16[2048,128]{1,0:T(8,128)(2,1)S(1)} fusion(bf16[2048,2048]{1,0:T(8,128)(2,1)} %fusion.12, bf16[2048,128]{1,0:T(8,128)(2,1)S(1)} %all_gather.26), kind=kOutput, calls=%fused_computation.31 | convolution fusion | flops 1074003968 | bytes 9437184 | tf_op jit(solution)/shard_map/dot_general | solution.py:94
  63.6 2.4 convolution_convert_fusion.3
  66.0 17.7 %all_gather.24 = bf16[2048,128]{1,0:T(8,128)(2,1)S(1)} all-gather(bf16[128,128]{1,0:T(8,128)(2,1)S(1)} %copy-done.3), channel_id=1, replica_groups=mesh['dp'=8,'fsdp'=16,'tensor'=2] {'fsdp'}, dimensions={0}, use_global_device_ids=true | all-gather | bytes 557056 | tf_op jit(solution)/shard_map/all_gather | solution.py:88
  83.7 2.4 convolution_convert_fusion.4
  86.1 17.5 %while.11 = (s32[]{:T(128)}, bf16[4,512,128]{2,1,0:T(8,128)(2,1)S(1)}, s32[4]{0:T(128)S(1)}, s32[2048]{0:T(1024)S(1)}, bf16[2048,128]{1,0:T(8,128)(2,1)S(1)}, /*...) while((s32[]{:T(128)}, ...), condition=%wide.region_4.5_spmd.clone, body=%wide.region_1.4_spmd.clone.sunk | while | flops 548470272 | bytes 13922487 | solution.py:43
  87.5 1.3 fusion.53
  89.5 0.9 fusion.55
  91.8 1.4 fusion.53
  96.2 1.4 fusion.53
  100.6 1.4 fusion.53
  103.6 17.4 %all_gather.27 = bf16[128,2048]{1,0:T(8,128)(2,1)S(1)} all-gather(bf16[128,128]{1,0:T(8,128)(2,1)S(1)} %copy-done.4), channel_id=1, replica_groups=mesh['dp'=8,'fsdp'=16,'tensor'=2] {'fsdp'}, dimensions={1}, use_global_device_ids=true | all-gather | bytes 557056 | tf_op jit(solution)/shard_map/all_gather | solution.py:106
  121.0 5.6 convolution_convert_fusion.1
  126.6 12.3 %copy.14 = bf16[2048,2048]{0,1:T(8,128)(2,1)} copy(bf16[2048,2048]{1,0:T(8,128)(2,1)} %convolution_convert_fusion.1) | data formatting | bytes 16777216
  139.6 89.4 %reduce-scatter.7.cloned.1.call-done = bf16[128,2048]{1,0:T(8,128)(2,1)} async-done(((bf16[2048,2048]{1,0:T(8,128)(2,1)}), bf16[128,2048]{1,0:T(8,128)(2,1)}) %reduce-scatter.7.cloned.1.call-update) | async-done | bytes 524304
  229.0 1.3 copy.15
  230.3 2.0 add_convert_fusion
  232.3 6.2 %gather_fusion = bf16[2048,128]{1,0:T(8,128)(2,1)S(1)} fusion(bf16[2048,128]{1,0:T(8,128)(2,1)S(1)} %get-tuple-element.79, s32[2048]{0:T(1024)S(1)} %get-tuple-element.83), kind=kCustom, calls=%fused_computation.clone | custom fusion | bytes 1056768 | tf_op jit(solution)/shard_map/jit(_take)/gather | solution.py:116
  241.7 53.7 %all-gather.5.cloned.1.call-done = bf16[1280,2048]{1,0:T(8,128)(2,1)} async-done(((bf16[1280,128]{1,0:T(8,128)(2,1)}), bf16[1280,2048]{1,0:T(8,128)(2,1)}) %all-gather.5.cloned.1.call-update) | async-done | bytes 5242896 | tf_op jit(solution)/shard_map/all_gather | solution.py:48
  295.4 3.6 fusion.13
  299.0 45.6 %all-gather.7.cloned.1.call-done = bf16[2048,512]{1,0:T(8,128)(2,1)} async-done(((bf16[128,512]{1,0:T(8,128)(2,1)}), bf16[2048,512]{1,0:T(8,128)(2,1)}) %all-gather.7.cloned.1.call-update) | async-done | bytes 2097168 | tf_op jit(solution)/shard_map/all_gather | solution.py:52
  344.6 7.6 %fusion.18 = f32[1280,512]{1,0:T(8,128)} fusion(bf16[2048,512]{1,0:T(8,128)(2,1)} %all-gather.7.cloned.1.call-done, bf16[1280,2048]{1,0:T(8,128)(2,1)} %all-gather.5.cloned.1.call-done, f32[2048]{0:T(1024)S(1)} %copy-done.8, f32[1280]{0:T(1024)S(1)} %add_rsqrt_fusion), kind=kOutput, calls=%fused_computation.34 | convolution fusion | flops 2694840320 | bytes 9974784 | tf_op jit(solution)/shard_map/dot_general | solution.py:50
  352.2 46.0 %all-gather.11.cloned.1.call-done = bf16[512,2048]{1,0:T(8,128)(2,1)} async-done(((bf16[512,128]{1,0:T(8,128)(2,1)}), bf16[512,2048]{1,0:T(8,128)(2,1)}) %all-gather.11.cloned.1.call-update) | async-done | bytes 2097168 | tf_op jit(solution)/shard_map/all_gather | solution.py:63
  398.3 51.7 %all-gather.9.cloned.1.call-done = bf16[2048,512]{1,0:T(8,128)(2,1)} async-done(((bf16[128,512]{1,0:T(8,128)(2,1)}), bf16[2048,512]{1,0:T(8,128)(2,1)}) %all-gather.9.cloned.1.call-update) | async-done | bytes 2097168 | tf_op jit(solution)/shard_map/all_gather | solution.py:57
  450.0 11.2 %convolution_convert_fusion = bf16[1280,2048]{1,0:T(8,128)(2,1)} fusion(bf16[512,2048]{1,0:T(8,128)(2,1)} %all-gather.11.cloned.1.call-done, bf16[2048,512]{1,0:T(8,128)(2,1)} %all-gather.9.cloned.1.call-done, f32[1280,512]{1,0:T(8,128)} %fusion.18, bf16[1280,2048]{1,0:T(8,128)(2,1)} %all-gather.5.cloned.1.call-done, f32[2048]{0:T(1024)S(1)} %copy-done.8, ...), kind=kOutput, calls=%fused_computation.27 | convolution fusion | flops 5385748480 | bytes 17314816 | tf_op jit(solution)/shard_map/dot_general | solution.py:61
  461.2 7.9 %copy.16 = bf16[1280,2048]{0,1:T(8,128)(2,1)} copy(bf16[1280,2048]{1,0:T(8,128)(2,1)} %convolution_convert_fusion) | data formatting | bytes 10485760
  470.9 61.5 %reduce-scatter.9.cloned.1.call-done = bf16[128,1280]{1,0:T(8,128)(2,1)} async-done(((bf16[2048,1280]{1,0:T(8,128)(2,1)}), bf16[128,1280]{1,0:T(8,128)(2,1)}) %reduce-scatter.9.cloned.1.call-update) | async-done | bytes 327696
  532.4 1.2 copy.17
  533.6 23.4 %scatter_custom_fusion = bf16[2048,128]{1,0:T(8,128)(2,1)} fusion(bf16[2048,128]{1,0:T(8,128)(2,1)} %get-tuple-element.80, s32[2048]{0:T(1024)S(1)} %get-tuple-element.84, bf16[768,128]{1,0:T(8,128)(2,1)S(1)} %slice.13, bf16[]{:T(256)} %constant.75, bf16[1280,128]{1,0:T(8,128)(2,1)S(1)} %add_convert_fusion.1, pred[2048]{0:T(1024)(128)(4,1)S(1)} %compare_and_fusion, ...), kind=kCustom, calls=%fused_computation.39 | custom fusion | flops 1572864 | bytes 1585156 | tf_op jit(solution)/shard_map/scatter | solution.py:128
  (63 shorter events, 14.3 us)
Async XLA Ops:
  6.5 5.1 copy-start.1
  6.5 25.1 %copy-start.2 = (bf16[128,128]{1,0:T(8,128)(2,1)S(1)}, bf16[128,128]{1,0:T(8,128)(2,1)}, u32[]{:S(2)}) copy-start(bf16[128,128]{1,0:T(8,128)(2,1)} %param.24) | copy-start | bytes 98308
  6.5 42.6 %copy-start.7 = (f32[2048]{0:T(1024)S(1)}, f32[2048]{0:T(1024)}, u32[]{:S(2)}) copy-start(f32[2048]{0:T(1024)} %param.21) | copy-start | bytes 24580
  6.5 222.4 %reduce-scatter.7.cloned.1.call-start = ((), (), s32[]{:S(2)}) async-start(), calls=%async_computation.6 | async-start | bytes 8912896
  57.7 5.9 %copy-start = (bf16[2048,2048]{1,0:T(8,128)(2,1)S(1)}, bf16[2048,2048]{1,0:T(8,128)(2,1)}, u32[]{:S(2)}) copy-start(bf16[2048,2048]{1,0:T(8,128)(2,1)} %fusion.12) | copy-start | bytes 25165828
  63.6 2.4 copy-start.3
  83.7 2.4 copy-start.6
  86.1 17.5 %copy-start.4 = (bf16[128,128]{1,0:T(8,128)(2,1)S(1)}, bf16[128,128]{1,0:T(8,128)(2,1)}, u32[]{:S(2)}) copy-start(bf16[128,128]{1,0:T(8,128)(2,1)} %param.26) | copy-start | bytes 98308
  138.9 0.7 copy-start.5
  138.9 156.5 %all-gather.5.cloned.1.call-start = ((), (), s32[]{:S(2)}) async-start(), calls=%async_computation.2 | async-start | bytes 5570560 | tf_op jit(solution)/shard_map/all_gather | solution.py:48
  232.3 112.3 %copy-start.8 = (f32[2048]{0:T(1024)S(1)}, f32[2048]{0:T(1024)}, u32[]{:S(2)}) copy-start(f32[2048]{0:T(1024)} %param.22) | copy-start | bytes 24580
  239.6 105.1 %all-gather.7.cloned.1.call-start = ((), (), s32[]{:S(2)}) async-start(), calls=%async_computation.3 | async-start | bytes 2228224 | tf_op jit(solution)/shard_map/all_gather | solution.py:52
  240.3 158.0 %all-gather.11.cloned.1.call-start = ((), (), s32[]{:S(2)}) async-start(), calls=%async_computation.5 | async-start | bytes 2228224 | tf_op jit(solution)/shard_map/all_gather | solution.py:63
  240.9 209.1 %all-gather.9.cloned.1.call-start = ((), (), s32[]{:S(2)}) async-start(), calls=%async_computation.4 | async-start | bytes 2228224 | tf_op jit(solution)/shard_map/all_gather | solution.py:57
  241.5 290.9 %reduce-scatter.9.cloned.1.call-start = ((), (), s32[]{:S(2)}) async-start(), calls=%async_computation.7 | async-start | bytes 5570560
  469.0 0.7 copy-start.9
Sparse Core Ops, SparseCore 0:
  139.0 89.9 reduce-scatter.6
  239.7 55.6 all-gather.4
  297.9 46.7 all-gather.6
  346.9 51.3 all-gather.10
  400.6 49.3 all-gather.8
  469.2 63.1 reduce-scatter.8
where the time goes:
time: 567 us; the launch traced here: 564 us
  waiting for transfers between devices  350 us (62%)
  blocking collectives  72.5 us (13%)
  other arithmetic  46.5 us (8%)
  matrix products  44.3 us (8%)
  local copies, waits for them, and re-layouts  34.2 us (6%)
  between operations  13.7 us (2%)
    unnamed x8, waiting for transfers between devices  153 us
    all_gather x1, waiting for transfers between devices, feed_forward(): lax.all_gather(ordered_cols, ('dp', 'tensor'), axis=1, tiled=True)  53.7 us
    all_gather x1, waiting for transfers between devices, feed_forward(): lax.all_gather(up_weight, 'fsdp', axis=0, tiled=True)  51.7 us
    all_gather x1, waiting for transfers between devices, feed_forward(): lax.all_gather(down_weight, 'fsdp', axis=1, tiled=True)  46 us
    all_gather x1, waiting for transfers between devices, feed_forward(): lax.all_gather(gate_weight, 'fsdp', axis=0, tiled=True)  45.6 us
    unnamed x24, local copies, waits for them, and re-layouts  23.9 us
    scatter x1, other arithmetic, body(): return own_cols.at[row_order].set(mixed)  23.4 us
    all_gather x1, blocking collectives, body(): lax.all_gather(value_weight, 'fsdp', axis=0, tiled=True)  20 us
  transfers between devices with their start and end apart: 6, of which 6 were waited for; matrix products, arithmetic and copies ran while one was open for 2% of the time, Pallas kernels for 0%

commit v1 on v0

v1 whole, which is shorter than its diff:
```python
import math

import jax
import jax.numpy as jnp
from jax import lax
from jax.experimental import pallas as pl
from jax.experimental.pallas import tpu as pltpu
from jax.sharding import PartitionSpec as P

F32 = jnp.float32
BF16 = jnp.bfloat16
NZ = 8
NX = 4
NY = 4
B = 128
ROWS = 2048
D = 2048
CAP = 1280
HALF = 640
QTR = 320
NBLK = 16
GROUPS = ((0, 3), (3, 4), (4, 12), (12, 16))
PER_GROUP = 17


def column_of(row):
    return jnp.transpose(jnp.broadcast_to(row, (B, B)))


def kernel(
    tok_hbm, seg_ref, ord_ref, cnt_ref, g1_ref, g2_ref,
    wq, wk, wv, wo, wg, wu, wd,
    out_ref,
    W, X, wqkv, q, k, v, att, ATT, SND, tokc, tokl,
    RS1, RB1, AGB, LHS, SS, ACC, H, RS2, RB2, FIN, FSND, segf, ordf, ordm,
    lsem, wsend, wrecv, z_send, z_recv, dsend, drecv,
):
    z = lax.axis_index("dp")
    j = lax.axis_index("fsdp")
    c = lax.axis_index("tensor")
    x = j // NY
    y = lax.rem(j, NY)
    xp = lax.rem(x + 1, NX)
    xm = lax.rem(x + NX - 1, NX)
    yp = lax.rem(y + 1, NY)
    ym = lax.rem(y + NY - 1, NY)
    zp = lax.rem(z + 1, NZ)
    zm = lax.rem(z + NZ - 1, NZ)
    dev_xp = {"fsdp": xp * NY + y}
    dev_xm = {"fsdp": xm * NY + y}
    dev_yp = {"fsdp": x * NY + yp}
    dev_ym = {"fsdp": x * NY + ym}
    dev_zp = {"dp": zp}
    dev_zm = {"dp": zm}
    dev_c = {"tensor": 1 - c}

    own = W.at[x, y, c]
    local = []
    for i, (ref) in enumerate((wq, wk, wv, wo)):
        local.append(pltpu.make_async_copy(ref, own.at[i], lsem.at[i]))
    for i in range(4):
        local.append(pltpu.make_async_copy(wg.at[:, pl.ds(i * B, B)], own.at[4 + i], lsem.at[4 + i]))
    for i in range(4):
        local.append(pltpu.make_async_copy(wu.at[:, pl.ds(i * B, B)], own.at[8 + i], lsem.at[8 + i]))
    for i in range(4):
        local.append(pltpu.make_async_copy(wd.at[pl.ds(i * B, B), :], own.at[12 + i], lsem.at[12 + i]))
    for i in range(3):
        local[i].start()
    tok = [
        pltpu.make_async_copy(
            tok_hbm.at[pl.ds(i * 256, 256), :], X.at[pl.ds(i * 256, 256), :], lsem.at[16 + i]
        )
        for i in range(8)
    ]
    for i in range(8):
        tok[i].start()
    for i in range(3, 16):
        local[i].start()
    tc = pltpu.make_async_copy(
        tok_hbm.at[:, pl.ds(pl.multiple_of(z * 256, 256), 256)], tokc, lsem.at[24]
    )
    tc.start()

    barrier = pltpu.get_barrier_semaphore()
    for dev in (dev_xp, dev_xm, dev_yp, dev_ym, dev_zp, dev_zm, dev_c):
        pl.semaphore_signal(barrier, inc=1, device_id=dev, device_id_type=pl.DeviceIdType.MESH)
    pl.semaphore_wait(barrier, 7)

    sent = []

    def remote(src, dst, ss, rs, dev):
        return pltpu.make_async_remote_copy(
            src_ref=src, dst_ref=dst, send_sem=ss, recv_sem=rs,
            device_id=dev, device_id_type=pl.DeviceIdType.MESH,
        )

    def go(cp):
        cp.start()
        sent.append(cp)

    def plan(g):
        a, b = GROUPS[g]
        nb = pl.ds(a, b - a)

        def cp(i, idx, dev):
            ref = W.at[idx]
            n = g * PER_GROUP + i
            return remote(ref, ref, wsend.at[n], wrecv.at[n], dev)

        alla = pl.ds(0, 64)
        allb = pl.ds(64, 64)
        full = pl.ds(0, 4)
        lo, hi = pl.ds(0, 2), pl.ds(2, 2)
        copies = [
            cp(0, (x, y, c, nb, alla), dev_xp),
            cp(1, (x, y, c, nb, alla), dev_xm),
            cp(2, (x, y, c, nb, allb), dev_yp),
            cp(3, (x, y, c, nb, allb), dev_ym),
            cp(4, (xm, y, c, nb, pl.ds(0, 32)), dev_xp),
            cp(5, (xp, y, c, nb, pl.ds(32, 32)), dev_xm),
            cp(6, (x, ym, c, nb, pl.ds(64, 32)), dev_yp),
            cp(7, (x, yp, c, nb, pl.ds(96, 32)), dev_ym),
            cp(8, (full, y, c, nb, alla), dev_yp),
            cp(9, (full, y, c, nb, alla), dev_ym),
            cp(10, (x, full, c, nb, allb), dev_xp),
            cp(11, (x, full, c, nb, allb), dev_xm),
            cp(12, (lo, ym, c, nb, alla), dev_yp),
            cp(13, (hi, yp, c, nb, alla), dev_ym),
            cp(14, (xm, lo, c, nb, allb), dev_xp),
            cp(15, (xp, hi, c, nb, allb), dev_xm),
        ]
        if g > 0:
            copies.append(cp(16, (full, full, c, nb), dev_c))

        def stage(s):
            if s == 0:
                for i in range(a, b):
                    local[i].wait()
            elif s <= 4:
                for i in range(4 * s - 4, 4 * s):
                    copies[i].wait_recv()
            if s < 4:
                for i in range(4 * s, 4 * s + 4):
                    go(copies[i])
            elif s == 4 and g > 0:
                go(copies[16])
            elif s == 5:
                copies[16].wait_recv()

        return stage

    gathers = [plan(g) for g in range(4)]

    segf[...] = seg_ref[...].astype(F32)
    order = ord_ref[...].astype(F32)
    ordf[...] = order
    rank = lax.broadcasted_iota(jnp.int32, (NBLK, B), 0) * B + lax.broadcasted_iota(
        jnp.int32, (NBLK, B), 1
    )
    ordm[...] = jnp.where(rank < cnt_ref[j], order, -1.0)
    gain1 = jnp.concatenate([g1_ref[pl.ds(i, 1), :] for i in range(NBLK)], axis=1)

    def norm_chunk(i):
        tok[i].wait()

        def body(r, _):
            rows = pl.ds(pl.multiple_of(i * 256 + r * 16, 16), 16)
            f = X[rows, :].astype(F32)
            inv = lax.rsqrt(jnp.mean(f * f, axis=-1, keepdims=True) + 1e-05)
            X[rows, :] = (f * inv * gain1).astype(BF16)
            return 0

        lax.fori_loop(0, 16, body, 0, unroll=2)

    gathers[0](0)
    norm_chunk(0)
    norm_chunk(1)
    gathers[0](1)
    norm_chunk(2)
    norm_chunk(3)
    gathers[0](2)
    norm_chunk(4)
    norm_chunk(5)
    norm_chunk(6)
    norm_chunk(7)
    gathers[0](3)
    gathers[1](0)
    gathers[0](4)
    gathers[2](0)

    def fill(jj, _):
        for b in range(3):
            wqkv[pl.ds(pl.multiple_of(jj * B, B), B), pl.ds(b * B, B)] = W[
                jj // NY, lax.rem(jj, NY), c, b
            ]
        return 0

    lax.fori_loop(0, 16, fill, 0)

    def qkv_tile(m, _):
        rows = pl.ds(pl.multiple_of(m * 256, 256), 256)
        r = jnp.dot(X[rows, :], wqkv[...], preferred_element_type=F32).astype(BF16)
        q[rows, :] = r[:, 0:B]
        k[rows, :] = r[:, B : 2 * B]
        v[rows, :] = r[:, 2 * B : 3 * B]
        return 0

    lax.fori_loop(0, 2, qkv_tile, 0)
    gathers[1](1)
    lax.fori_loop(2, 4, qkv_tile, 0)
    gathers[1](2)
    gathers[2](1)
    lax.fori_loop(4, 8, qkv_tile, 0)
    gathers[1](3)
    gathers[2](2)

    scale = 1.0 / math.sqrt(B)

    def att_block(i, _):
        st = jnp.maximum(i - 4, 0)
        qrows = pl.ds(pl.multiple_of(i * B, B), B)
        krows = pl.ds(pl.multiple_of(st * B, B), 5 * B)
        s = (
            lax.dot_general(
                q[qrows, :], k[krows, :], (((1,), (1,)), ((), ())), preferred_element_type=F32
            )
            * scale
        )
        segq = column_of(segf[pl.ds(i, 1), :])
        segq = jnp.concatenate([segq] * 5, axis=1)
        segk = jnp.concatenate([segf[pl.ds(st + t, 1), :] for t in range(5)], axis=1)
        diff = lax.broadcasted_iota(jnp.int32, (B, 5 * B), 0) - lax.broadcasted_iota(
            jnp.int32, (B, 5 * B), 1
        )
        allowed = (segq == segk) & (diff >= (st - i) * B)
        s = jnp.where(allowed, s, -1e30)
        e = jnp.exp(s - jnp.max(s, axis=-1, keepdims=True))
        p = (e * (1.0 / jnp.sum(e, axis=-1, keepdims=True))).astype(BF16)
        att[qrows, :] = jnp.dot(p, v[krows, :], preferred_element_type=F32).astype(BF16)
        return 0

    lax.fori_loop(0, 8, att_block, 0)
    gathers[1](4)
    lax.fori_loop(8, 16, att_block, 0)

    lane = lax.broadcasted_iota(jnp.int32, (B, B), 1).astype(F32)
    sub = lax.broadcasted_iota(jnp.int32, (B, B), 0).astype(F32)

    def one_hot(rb):
        col = column_of(ordf[pl.ds(rb, 1), :])
        return jnp.concatenate(
            [jnp.where(col == lane + (B * u), 1.0, 0.0).astype(BF16) for u in range(NBLK)], axis=1
        )

    def pick_other(t, _):
        oh = one_hot((1 - c) * 5 + t)
        SND[pl.ds(pl.multiple_of(t * B, B), B), :] = jnp.dot(
            oh, att[...], preferred_element_type=F32
        ).astype(BF16)
        return 0

    lax.fori_loop(0, 5, pick_other, 0)
    swap = remote(SND, ATT.at[c], dsend.at[0], drecv.at[0], dev_c)
    go(swap)
    tc.wait()

    def pick_own(t, _):
        oh = one_hot(c * 5 + t)
        rows = pl.ds(pl.multiple_of(t * B, B), B)
        ATT[c, rows, :] = jnp.dot(oh, att[...], preferred_element_type=F32).astype(BF16)
        tokl[rows, :] = jnp.dot(oh, tokc[...], preferred_element_type=F32).astype(BF16)
        return 0

    lax.fori_loop(0, 5, pick_own, 0)
    gathers[1](5)
    swap.wait_recv()

    def w_index(zs):
        return zs // 2, 2 * lax.rem(zs, 2)

    def ring_copy(base, src, dst, d, s, h):
        n = base + (d * 4 + s) * 2 + h
        return remote(src, dst, z_send.at[n], z_recv.at[n], dev_zp if d == 0 else dev_zm)

    def reduce_ring(base, R, RB, partial, finish, extras):
        copies = {}
        for d in (0, 1):
            far = lax.rem(z + 4, NZ)
            RB[d] = partial(far, d).astype(BF16)
            copies[d, 0, d] = ring_copy(base, RB.at[d], R.at[d, 0, d], d, 0, d)
            go(copies[d, 0, d])
        for s in (1, 2, 3):
            order_h = ((0, 1), (1, 0), (0, 0), (1, 1)) if s == 1 else ((0, 0), (1, 1), (0, 1), (1, 0))
            if s > 1:
                order_h = ((0, 1), (1, 0), (0, 0), (1, 1))
            for d, h in order_h:
                dest = lax.rem(z + 4 - s, NZ) if d == 0 else lax.rem(z + 4 + s, NZ)
                part = partial(dest, h)
                slot = R.at[d, s - 1, h]
                if (d, s - 1, h) in copies:
                    copies[d, s - 1, h].wait_recv()
                    part = part + slot[...].astype(F32)
                slot[...] = part.astype(BF16)
                copies[d, s, h] = ring_copy(base, slot, R.at[d, s, h], d, s, h)
                go(copies[d, s, h])
            for f in extras.get(s, ()):
                f()
        for h in (1, 0):
            part = partial(z, h)
            copies[0, 3, h].wait_recv()
            copies[1, 3, h].wait_recv()
            finish(h, part + R[0, 3, h].astype(F32) + R[1, 3, h].astype(F32))

    def rows_of(h):
        return pl.ds(h * QTR, QTR)

    def head_partial(zd, h):
        xw, yw = w_index(zd)
        rhs = jnp.concatenate(
            [
                jnp.concatenate([W[xw, yw + e, cc, 3] for e in range(2)], axis=1)
                for cc in range(2)
            ],
            axis=0,
        )
        lhs = jnp.concatenate([ATT[0, rows_of(h), :], ATT[1, rows_of(h), :]], axis=1)
        return jnp.dot(lhs, rhs, preferred_element_type=F32)

    def head_finish(h, total):
        AGB[z, rows_of(h), :] = (tokl[rows_of(h), :].astype(F32) + total).astype(BF16)
        for d in (0, 1):
            go(ag_copy(d, 0, h))

    ag = {}

    def ag_copy(d, s, h):
        if (d, s, h) not in ag:
            src = lax.rem(z + NZ - s, NZ) if d == 0 else lax.rem(z + s, NZ)
            ref = AGB.at[src, rows_of(h)]
            ag[d, s, h] = ring_copy(16, ref, ref, d, s, h)
        return ag[d, s, h]

    reduce_ring(
        0, RS1, RB1, head_partial, head_finish,
        {
            1: (lambda: gathers[2](3),),
            2: (lambda: gathers[3](0),),
            3: (lambda: gathers[2](4), lambda: gathers[3](1)),
        },
    )

    def ff_in(zs, h, first):
        xw, yw = w_index(zs)
        rows = rows_of(h)
        f = AGB[zs, rows, :].astype(F32)
        sq = f * f
        sq = sq[:, :B] + sq[:, B:]
        SS[rows, :] = sq if first else SS[rows, :] + sq
        gain = jnp.concatenate([g2_ref[pl.ds(2 * zs + e, 1), :] for e in range(2)], axis=1)
        LHS[...] = (f * gain).astype(BF16)

        def body(n, _):
            cc = n // 2
            blk = 4 + 4 * lax.rem(n, 2)
            rhs = jnp.concatenate(
                [
                    jnp.concatenate([W[xw, yw + e, cc, blk + b] for b in range(4)], axis=1)
                    for e in range(2)
                ],
                axis=0,
            )
            prod = jnp.dot(LHS[...], rhs, preferred_element_type=F32)
            if first:
                ACC[n, rows, :] = prod
            else:
                ACC[n, rows, :] = ACC[n, rows, :] + prod
            return 0

        lax.fori_loop(0, 4, body, 0)

    gathers[3](2)
    gathers[2](5)
    ff_in(z, 1, True)
    ff_in(z, 0, True)
    for s in range(4):
        got = []
        for h in (1, 0):
            for d in (0, 1):
                if s == 3 and h != d:
                    continue
                ag_copy(d, s, h).wait_recv()
                got.append((d, h))
                if s < 2 or (s == 2 and h == d):
                    go(ag_copy(d, s + 1, h))
        if s == 0:
            gathers[3](3)
        if s == 1:
            gathers[3](4)
        for d, h in got:
            ff_in(lax.rem(z + NZ - 1 - s, NZ) if d == 0 else lax.rem(z + 1 + s, NZ), h, False)

    def act(r, _):
        rows = pl.ds(pl.multiple_of(r * 32, 32), 32)
        inv = lax.rsqrt(jnp.sum(SS[rows, :], axis=-1, keepdims=True) * (1.0 / D) + 1e-05)
        for cc in range(2):
            g = ACC[2 * cc, rows, :] * inv
            u = ACC[2 * cc + 1, rows, :] * inv
            H[rows, pl.ds(cc * 512, 512)] = (g / (1.0 + jnp.exp(-g)) * u).astype(BF16)
        return 0

    lax.fori_loop(0, HALF // 32, act, 0)
    gathers[3](5)

    def ff_partial(zd, h):
        xw, yw = w_index(zd)
        rhs = jnp.concatenate(
            [
                jnp.concatenate([W[xw, yw + e, cc, 12 + b] for e in range(2)], axis=1)
                for cc in range(2)
                for b in range(4)
            ],
            axis=0,
        )
        return jnp.dot(H[rows_of(h), :], rhs, preferred_element_type=F32)

    def ff_finish(h, total):
        fin = (AGB[z, rows_of(h), :].astype(F32) + total).astype(BF16)
        FIN[c, rows_of(h), :] = jnp.where(c == 0, fin[:, :B], fin[:, B:])
        FSND[rows_of(h), :] = jnp.where(c == 0, fin[:, B:], fin[:, :B])

    reduce_ring(32, RS2, RB2, ff_partial, ff_finish, {})
    swap2 = remote(FSND, FIN.at[c], dsend.at[1], drecv.at[1], dev_c)
    go(swap2)
    swap2.wait_recv()

    ones = jnp.ones((HALF, B), BF16)

    def put(t, _):
        rows = pl.ds(pl.multiple_of(t * B, B), B)
        base = (t * B).astype(F32)
        acc = jnp.zeros((B, 2 * B), F32)
        for half in range(2):
            oh = jnp.concatenate(
                [
                    jnp.where(ordm[pl.ds(half * 5 + u, 1), :] == sub + base, 1.0, 0.0).astype(BF16)
                    for u in range(5)
                ],
                axis=1,
            )
            acc = acc + jnp.dot(
                oh, jnp.concatenate([FIN[half], ones], axis=1), preferred_element_type=F32
            )
        old = tokc[rows, :]
        old = jnp.where(c == 0, old[:, :B], old[:, B:])
        out_ref[rows, :] = jnp.where(acc[:, B:] > 0.5, acc[:, :B], old.astype(F32)).astype(BF16)
        return 0

    lax.fori_loop(0, NBLK, put, 0)
    for cp in sent:
        cp.wait_send()


def body(
    tokens, segment_ids, row_order, row_counts, first_gain, second_gain,
    query_weight, key_weight, value_weight, output_weight, gate_weight, up_weight, down_weight,
):
    vm = pl.BlockSpec(memory_space=pltpu.VMEM)
    anyspace = pl.BlockSpec(memory_space=pl.ANY)
    smem = pl.BlockSpec(memory_space=pltpu.SMEM)
    return pl.pallas_call(
        kernel,
        out_shape=jax.ShapeDtypeStruct((ROWS, B), BF16),
        in_specs=[anyspace, vm, vm, smem, vm, vm] + [anyspace] * 7,
        out_specs=vm,
        scratch_shapes=[
            pltpu.VMEM((NX, NY, 2, NBLK, B, B), BF16),
            pltpu.VMEM((ROWS, D), BF16),
            pltpu.VMEM((D, 3 * B), BF16),
            pltpu.VMEM((ROWS, B), BF16),
            pltpu.VMEM((ROWS, B), BF16),
            pltpu.VMEM((ROWS, B), BF16),
            pltpu.VMEM((ROWS, B), BF16),
            pltpu.VMEM((2, HALF, B), BF16),
            pltpu.VMEM((HALF, B), BF16),
            pltpu.VMEM((ROWS, 2 * B), BF16),
            pltpu.VMEM((HALF, 2 * B), BF16),
            pltpu.VMEM((2, 4, 2, QTR, 2 * B), BF16),
            pltpu.VMEM((2, QTR, 2 * B), BF16),
            pltpu.VMEM((NZ, HALF, 2 * B), BF16),
            pltpu.VMEM((QTR, 2 * B), BF16),
            pltpu.VMEM((HALF, B), F32),
            pltpu.VMEM((4, HALF, 512), F32),
            pltpu.VMEM((HALF, 1024), BF16),
            pltpu.VMEM((2, 4, 2, QTR, 2 * B), BF16),
            pltpu.VMEM((2, QTR, 2 * B), BF16),
            pltpu.VMEM((2, HALF, B), BF16),
            pltpu.VMEM((HALF, B), BF16),
            pltpu.VMEM((NBLK, B), F32),
            pltpu.VMEM((NBLK, B), F32),
            pltpu.VMEM((NBLK, B), F32),
            pltpu.SemaphoreType.DMA((25,)),
            pltpu.SemaphoreType.DMA((4 * PER_GROUP,)),
            pltpu.SemaphoreType.DMA((4 * PER_GROUP,)),
            pltpu.SemaphoreType.DMA((48,)),
            pltpu.SemaphoreType.DMA((48,)),
            pltpu.SemaphoreType.DMA((2,)),
            pltpu.SemaphoreType.DMA((2,)),
        ],
        compiler_params=pltpu.CompilerParams(
            collective_id=0, has_side_effects=True, vmem_limit_bytes=66 * 1000 * 1000
        ),
        name="recursion_step",
    )(
        tokens,
        segment_ids.reshape(NBLK, B),
        row_order.reshape(NBLK, B),
        row_counts,
        first_gain.reshape(NBLK, B),
        second_gain.reshape(NBLK, B),
        query_weight, key_weight, value_weight, output_weight,
        gate_weight, up_weight, down_weight,
    )


def solution(mesh):
    weight = P("fsdp", ("dp", "tensor"))
    weight_t = P(("dp", "tensor"), "fsdp")
    in_specs = (
        P("fsdp", None), P("fsdp"), P("fsdp"), P(), P(), P(),
        weight, weight, weight, weight_t, weight, weight, weight_t,
    )
    return jax.shard_map(
        body, mesh=mesh, in_specs=in_specs, out_specs=weight, check_vma=False
    )
```

time: 567 us -> 151 us (0.27)
  waiting for transfers between devices: 350 us -> 0 us
  Pallas kernels: 0 us -> 149 us
  blocking collectives: 72.5 us -> 0 us
  other arithmetic: 46.5 us -> 0 us
  matrix products: 44.3 us -> 0 us
  local copies, waits for them, and re-layouts: 34.2 us -> 1.87 us
  between operations: 13.7 us -> 0.01 us
    all_gather x4 -> x0, waiting for transfers between devices: 197 us -> none  [the longest x1 53.7 us: feed_forward(): lax.all_gather(ordered_cols, ('dp', 'tensor'), axis=1, tiled=True)]
    unnamed x8 -> x0, waiting for transfers between devices: 153 us -> none
    pallas_call x0 -> x1, Pallas kernels: none -> 149 us  [body(): pl.pallas_call(kernel, out_shape=jax.ShapeDtypeStruct((ROWS, B), BF16), i...]
    all_gather x4 -> x0, blocking collectives: 72.5 us -> none  [the longest x1 20 us: body(): lax.all_gather(value_weight, 'fsdp', axis=0, tiled=True)]
    dot_general x14 -> x0, matrix products: 44.3 us -> none  [the longest x1 11.2 us: feed_forward(): jnp.dot(hidden, lax.all_gather(down_weight, 'fsdp', axis=1, tiled=True),...]
    scatter x1 -> x0, other arithmetic: 23.4 us -> none  [body(): return own_cols.at[row_order].set(mixed)]
    unnamed x24 -> x1, local copies, waits for them, and re-layouts: 23.9 us -> 1.87 us
    reduce_sum x6 -> x0, other arithmetic: 11.5 us -> none  [the longest x2 8.68 us: rms_scale(): jnp.mean(floats * floats, axis=-1, keepdims=True) + 1e-05]
  transfers between devices with their start and end apart: 6 -> 0, of which waited for: 6 -> 0; matrix products, arithmetic and copies ran while one was open for 2% -> 0% of each run, Pallas kernels for 0% -> 0%
where the time goes in v1:
time: 151 us
  Pallas kernels  149 us (99%)
  local copies, waits for them, and re-layouts  1.87 us (1%)
    pallas_call x1, Pallas kernels, body(): pl.pallas_call(kernel, out_shape=jax.ShapeDtypeStruct((ROWS, B), BF16), i...  149 us

profile of v1, /device:TPU:1, one launch (start us, length us, event | category | flops | bytes accessed | tf_op | source)
XLA Modules:
  0.0 150.7 jit_solution(16368238283706155850)
XLA Ops:
  0.0 148.9 %recursion_step.1 = bf16[2048,128]{1,0:T(8,128)(2,1)} custom-call(bf16[2048,2048]{1,0:T(8,128)(2,1)} %tok_hbm.1, s32[16,128]{1,0:T(8,128)} %bitcast.4, s32[16,128]{1,0:T(8,128)} %bitcast.5, s32[16]{0:T(128)} %cnt_ref.1, f32[16,128]{1,0:T(8,128)} %bitcast.6, f32[16,128]{1,0:T(8,128)} %bitcast.7, bf16[128,128]{1,0:T(8,128)(2,1)} %wq.1, bf16[128,128]{1,0:T(8,128)(2,1)} %wk.1, ...), custom_call_target="tpu_custom_call" | custom-call | tf_op jit(solution)/shard_map/recursion_step/pallas_call | solution.py:470
  148.9 1.9 %copy.15 = bf16[2048,128]{1,0:T(8,128)(2,1)} copy(bf16[2048,128]{1,0:T(8,128)(2,1)} %recursion_step.1) | data formatting | bytes 1048576

commit v2 on v1

v2 whole, which is shorter than its diff:
```python
import math

import jax
import jax.numpy as jnp
from jax import lax
from jax.experimental import pallas as pl
from jax.experimental.pallas import tpu as pltpu
from jax.sharding import PartitionSpec as P

F32 = jnp.float32
BF16 = jnp.bfloat16
NZ = 8
NX = 4
NY = 4
B = 128
ROWS = 2048
D = 2048
HALF = 640
QTR = 320
NBLK = 16
PIECE = 80
O_AT, G_AT, U_AT, D_AT, BLOCKS = 3, 11, 15, 19, 23
GROUPS = ((0, 3), (3, 11), (11, 19), (19, 23))
PER_GROUP = 29


def column_of(row):
    return jnp.transpose(jnp.broadcast_to(row, (B, B)))


def kernel(
    tok_hbm, seg_ref, ord_ref, cnt_ref, g1_ref, g2_ref,
    wq, wk, wv, wo, wg, wu, wd,
    out_ref,
    W, X, XN, q, k, v, att, OHP, PICK, A2, AGB, NRM, H, RS2, RB2, FIN, FSND, P1, LIVE,
    segf, ordf, ordm,
    lsem, wsend, wrecv, z_send, z_recv, dsend, drecv,
):
    z = lax.axis_index("dp")
    j = lax.axis_index("fsdp")
    c = lax.axis_index("tensor")
    x = j // NY
    y = lax.rem(j, NY)
    xp = lax.rem(x + 1, NX)
    xm = lax.rem(x + 3, NX)
    x2 = lax.rem(x + 2, NX)
    yp = lax.rem(y + 1, NY)
    ym = lax.rem(y + 3, NY)
    y2 = lax.rem(y + 2, NY)
    dev_xp = {"fsdp": xp * NY + y}
    dev_xm = {"fsdp": xm * NY + y}
    dev_yp = {"fsdp": x * NY + yp}
    dev_ym = {"fsdp": x * NY + ym}
    dev_c = {"tensor": 1 - c}

    def z_at(step):
        return lax.rem(z + step, NZ)

    def dev_z(step, other=0):
        if other:
            return {"dp": z_at(step), "tensor": 1 - c}
        return {"dp": z_at(step)}

    barrier = pltpu.get_barrier_semaphore()
    peers = [dev_xp, dev_xm, dev_yp, dev_ym, dev_c]
    peers += [dev_z(dz, other) for dz in range(1, NZ) for other in (0, 1)]
    for dev in peers:
        pl.semaphore_signal(barrier, inc=1, device_id=dev, device_id_type=pl.DeviceIdType.MESH)

    own = W.at[x, y, c]
    spots = [(wq, 0), (wk, 1), (wv, 2), (wo, O_AT + z)]
    spots += [(wg.at[:, pl.ds(i * B, B)], G_AT + i) for i in range(4)]
    spots += [(wu.at[:, pl.ds(i * B, B)], U_AT + i) for i in range(4)]
    spots += [(wd.at[pl.ds(i * B, B), :], D_AT + i) for i in range(4)]
    local = [pltpu.make_async_copy(ref, own.at[b], lsem.at[i]) for i, (ref, b) in enumerate(spots)]
    local_of = ((0, 3), (3, 4), (4, 12), (12, 16))
    for i in range(4):
        local[i].start()
    tok = [
        pltpu.make_async_copy(
            tok_hbm.at[pl.ds(i * 256, 256), :], X.at[pl.ds(i * 256, 256), :], lsem.at[16 + i]
        )
        for i in range(8)
    ]
    for i in range(8):
        tok[i].start()
    for i in range(4, 16):
        local[i].start()

    pl.semaphore_wait(barrier, len(peers))

    sent = []

    def remote(src, dst, ss, rs, dev):
        return pltpu.make_async_remote_copy(
            src_ref=src, dst_ref=dst, send_sem=ss, recv_sem=rs,
            device_id=dev, device_id_type=pl.DeviceIdType.MESH,
        )

    def go(cp):
        cp.start()
        sent.append(cp)

    def plan(g):
        a, b = GROUPS[g]
        nb = pl.ds(a, b - a)
        up, dn = pl.ds(0, 64), pl.ds(64, 64)
        full = pl.ds(0, 4)
        lo, hi = pl.ds(0, 2), pl.ds(2, 2)

        def cp(i, idx, dev):
            ref = W.at[idx]
            n = g * PER_GROUP + i
            return remote(ref, ref, wsend.at[n], wrecv.at[n], dev)

        copies = [
            ((x, y, c, nb, up), dev_xp),
            ((x, y, c, nb, up), dev_xm),
            ((x, y, c, nb, dn), dev_yp),
            ((x, y, c, nb, dn), dev_ym),
            ((xm, y, c, nb, pl.ds(0, 32)), dev_xp),
            ((xp, y, c, nb, pl.ds(32, 32)), dev_xm),
            ((x, ym, c, nb, pl.ds(64, 32)), dev_yp),
            ((x, yp, c, nb, pl.ds(96, 32)), dev_ym),
            ((full, y, c, nb, up), dev_yp),
            ((full, y, c, nb, up), dev_ym),
            ((x, full, c, nb, dn), dev_xp),
            ((x, full, c, nb, dn), dev_xm),
            ((lo, ym, c, nb, up), dev_yp),
            ((hi, yp, c, nb, up), dev_ym),
            ((xm, lo, c, nb, dn), dev_xp),
            ((xp, hi, c, nb, dn), dev_xm),
        ]
        pass_on = (
            ((x, y, c, nb),),
            ((xm, y, c, nb, up), (xp, y, c, nb, up), (x, ym, c, nb, dn), (x, yp, c, nb, dn)),
            ((x2, y, c, nb, up), (x, y2, c, nb, dn)),
            ((full, ym, c, nb, up), (full, yp, c, nb, up), (xm, full, c, nb, dn), (xp, full, c, nb, dn)),
            ((full, y2, c, nb, up), (x2, full, c, nb, dn)),
        )
        first = (16, 17, 21, 23, 27)
        made = {}

        def stage(s):
            if s == 5:
                for i in range(16, 29):
                    made[i].wait_recv()
                return
            if s == 0:
                for i in range(*local_of[g]):
                    if i != 3:
                        local[i].wait()
            else:
                for i in range(4 * s - 4, 4 * s):
                    made[i].wait_recv()
            if s < 4:
                for i in range(4 * s, 4 * s + 4):
                    made[i] = cp(i, *copies[i])
                    go(made[i])
            if g > 0:
                for e, idx in enumerate(pass_on[s]):
                    i = first[s] + e
                    made[i] = cp(i, idx, dev_c)
                    go(made[i])

        return stage

    gathers = [plan(g) for g in range(4)]

    gathers[0](0)
    local[3].wait()
    o_piece = own.at[O_AT + z]
    o_copies = [
        remote(o_piece, o_piece, z_send.at[dz], z_recv.at[dz], dev_z(dz)) for dz in range(1, NZ)
    ]
    for cp in o_copies:
        go(cp)

    segf[...] = seg_ref[...].astype(F32)
    order = ord_ref[...].astype(F32)
    ordf[...] = order
    rank = lax.broadcasted_iota(jnp.int32, (NBLK, B), 0) * B + lax.broadcasted_iota(
        jnp.int32, (NBLK, B), 1
    )
    ordm[...] = jnp.where(rank < cnt_ref[j], order, -1.0)
    gain1 = jnp.concatenate([g1_ref[pl.ds(i, 1), :] for i in range(NBLK)], axis=1)
    gain2 = jnp.concatenate([g2_ref[pl.ds(i, 1), :] for i in range(NBLK)], axis=1)

    def normed(data, gain):
        f = data.astype(F32)
        inv = lax.rsqrt(jnp.mean(f * f, axis=-1, keepdims=True) + 1e-05)
        return (f * inv * gain).astype(BF16)

    def norm_chunk(i):
        tok[i].wait()

        def body(r, _):
            rows = pl.ds(pl.multiple_of(i * 256 + r * 16, 16), 16)
            XN[rows, :] = normed(X[rows, :], gain1)
            return 0

        lax.fori_loop(0, 16, body, 0, unroll=4)

    lane = lax.broadcasted_iota(jnp.int32, (B, B), 1).astype(F32)
    sub = lax.broadcasted_iota(jnp.int32, (B, B), 0).astype(F32)

    def one_hot(t, _):
        rows = pl.ds(pl.multiple_of(t * B, B), B)
        col = column_of(ordf[pl.ds(t, 1), :])
        for u in range(NBLK):
            OHP[rows, pl.ds(u * B, B)] = jnp.where(col == lane + (B * u), 1.0, 0.0).astype(BF16)
        return 0

    norm_chunk(0)
    norm_chunk(1)
    norm_chunk(2)
    gathers[0](1)
    norm_chunk(3)
    norm_chunk(4)
    gathers[0](2)
    norm_chunk(5)
    norm_chunk(6)
    norm_chunk(7)
    lax.fori_loop(0, 10, one_hot, 0)
    gathers[0](3)
    for cp in o_copies:
        cp.wait_recv()
    gathers[1](0)
    gathers[0](4)

    def blocks(cc, b, count):
        return jnp.concatenate(
            [
                jnp.concatenate([W[i // NY, i % NY, cc, b + e] for e in range(count)], axis=1)
                for i in range(16)
            ],
            axis=0,
        )

    def qkv_tile(m, _):
        rows = pl.ds(pl.multiple_of(m * 256, 256), 256)
        r = jnp.dot(XN[rows, :], blocks(c, 0, 3), preferred_element_type=F32).astype(BF16)
        q[rows, :] = r[:, 0:B]
        k[rows, :] = r[:, B : 2 * B]
        v[rows, :] = r[:, 2 * B : 3 * B]
        return 0

    lax.fori_loop(0, 5, qkv_tile, 0)
    gathers[1](1)
    gathers[2](0)
    lax.fori_loop(5, 8, qkv_tile, 0)

    scale = 1.0 / math.sqrt(B)

    def att_block(i, _):
        st = jnp.maximum(i - 4, 0)
        qrows = pl.ds(pl.multiple_of(i * B, B), B)
        krows = pl.ds(pl.multiple_of(st * B, B), 5 * B)
        s = (
            lax.dot_general(
                q[qrows, :], k[krows, :], (((1,), (1,)), ((), ())), preferred_element_type=F32
            )
            * scale
        )
        segq = column_of(segf[pl.ds(i, 1), :])
        segq = jnp.concatenate([segq] * 5, axis=1)
        segk = jnp.concatenate([segf[pl.ds(st + t, 1), :] for t in range(5)], axis=1)
        diff = lax.broadcasted_iota(jnp.int32, (B, 5 * B), 0) - lax.broadcasted_iota(
            jnp.int32, (B, 5 * B), 1
        )
        allowed = (segq == segk) & (diff >= (st - i) * B)
        s = jnp.where(allowed, s, -1e30)
        e = jnp.exp(s - jnp.max(s, axis=-1, keepdims=True))
        p = (e * (1.0 / jnp.sum(e, axis=-1, keepdims=True))).astype(BF16)
        att[qrows, :] = jnp.dot(p, v[krows, :], preferred_element_type=F32).astype(BF16)
        return 0

    lax.fori_loop(0, 4, att_block, 0, unroll=2)
    gathers[1](2)
    lax.fori_loop(4, 10, att_block, 0, unroll=2)
    gathers[2](1)
    lax.fori_loop(10, 16, att_block, 0, unroll=2)

    def pick(t, _):
        rows = pl.ds(pl.multiple_of(t * 256, 256), 256)
        PICK[rows, :] = jnp.dot(OHP[rows, :], att[...], preferred_element_type=F32).astype(BF16)
        return 0

    lax.fori_loop(0, 5, pick, 0)

    def piece_rows(zs, cc):
        return pl.ds(pl.multiple_of(cc * HALF + zs * PIECE, 16), PIECE)

    spread = []
    for dz in (4, 3, 5, 2, 6, 1, 7, 0):
        for other in (0, 1):
            if dz == 0 and other == 0:
                continue
            cc = 1 - c if other else c
            n = 8 + dz * 2 + other
            dev = dev_z(dz, other) if dz else dev_c
            spread.append(
                remote(
                    PICK.at[piece_rows(z_at(dz), cc)], A2.at[2 * z + c],
                    z_send.at[n], z_recv.at[n], dev,
                )
            )
            go(spread[-1])
    A2[2 * z + c] = PICK[piece_rows(z, c), :]

    def row_tokens(n, _):
        cols = pl.ds(pl.multiple_of(n * 256, 256), 256)
        AGB[z, :, cols] = jnp.dot(
            OHP[piece_rows(z, c), :], X[:, cols], preferred_element_type=F32
        ).astype(BF16)
        return 0

    lax.fori_loop(0, 8, row_tokens, 0)

    def put_hot(t, _):
        rows = pl.ds(pl.multiple_of(t * B, B), B)
        base = (t * B).astype(F32)
        for u in range(10):
            XN[rows, pl.ds(u * B, B)] = jnp.where(
                ordm[pl.ds(u, 1), :] == sub + base, 1.0, 0.0
            ).astype(BF16)
        return 0

    lax.fori_loop(0, 8, put_hot, 0)
    gathers[1](3)
    gathers[2](2)
    lax.fori_loop(8, 16, put_hot, 0)
    ones = jnp.ones((2 * HALF, B), BF16)

    def live(t, _):
        rows = pl.ds(pl.multiple_of(t * 256, 256), 256)
        LIVE[rows, :] = jnp.dot(
            XN[rows, pl.ds(0, 2 * HALF)], ones, preferred_element_type=F32
        ).astype(BF16)
        return 0

    lax.fori_loop(0, 8, live, 0)
    gathers[1](4)
    for cp in spread:
        cp.wait_recv()
    gathers[1](5)

    def w_index(n):
        return n // 2, 2 * lax.rem(n, 2)

    def ring_copy(base, src, dst, d, s, h):
        n = base + (d * 4 + s) * 2 + h
        return remote(src, dst, z_send.at[n], z_recv.at[n], dev_z(1) if d == 0 else dev_z(7))

    ag = {}

    def ag_copy(d, s, h):
        if (d, s, h) not in ag:
            src = z_at(NZ - s) if d == 0 else z_at(s)
            ref = AGB.at[src, :, pl.ds(h * 1024, 1024)]
            ag[d, s, h] = ring_copy(24, ref, ref, d, s, h)
        return ag[d, s, h]

    def out_proj(n, _):
        xw, yw = w_index(n)
        cols = pl.ds(pl.multiple_of(n * 256, 256), 256)
        rhs = jnp.concatenate(
            [
                jnp.concatenate([W[xw, yw + e, hh % 2, O_AT + hh // 2] for e in range(2)], axis=1)
                for hh in range(16)
            ],
            axis=0,
        )
        lhs = jnp.concatenate([A2[hh] for hh in range(16)], axis=1)
        total = jnp.dot(lhs, rhs, preferred_element_type=F32)
        AGB[z, :, cols] = (AGB[z, :, cols].astype(F32) + total).astype(BF16)
        return 0

    for h in (0, 1):
        lax.fori_loop(4 * h, 4 * h + 4, out_proj, 0)
        for d in (0, 1):
            go(ag_copy(d, 0, h))

    def prepare(i, zs):
        for r in range(0, PIECE, 16):
            NRM[pl.ds(i * PIECE + r, 16), :] = normed(AGB[zs, pl.ds(r, 16), :], gain2)

    def ff_in(sources):
        count = len(sources)

        def body(n, _):
            cc = n // 2
            e = 2 * lax.rem(n, 2)
            lhs = NRM[pl.ds(0, count * PIECE), :]
            g = jnp.dot(lhs, blocks(cc, G_AT + e, 2), preferred_element_type=F32)
            u = jnp.dot(lhs, blocks(cc, U_AT + e, 2), preferred_element_type=F32)
            hid = (g / (1.0 + jnp.exp(-g)) * u).astype(BF16)
            cols = pl.ds(pl.multiple_of(n * 256, 256), 256)
            for i, zs in enumerate(sources):
                H[pl.ds(pl.multiple_of(zs * PIECE, 16), PIECE), cols] = hid[
                    i * PIECE : (i + 1) * PIECE
                ]
            return 0

        lax.fori_loop(0, 4, body, 0)

    def receive(s):
        for h in (0, 1):
            for d in (0, 1):
                if s == 3 and h != d:
                    continue
                ag_copy(d, s, h).wait_recv()
                if s < 2 or (s == 2 and h == d):
                    go(ag_copy(d, s + 1, h))

    prepare(0, z)
    receive(0)
    prepare(1, z_at(1))
    prepare(2, z_at(7))
    gathers[2](3)
    gathers[3](0)
    receive(1)
    gathers[2](4)
    gathers[3](1)
    gathers[2](5)
    ff_in([z, z_at(1), z_at(7)])
    gathers[3](2)
    prepare(0, z_at(2))
    prepare(1, z_at(6))
    receive(2)
    ff_in([z_at(2), z_at(6)])
    gathers[3](3)
    prepare(0, z_at(3))
    prepare(1, z_at(5))
    ff_in([z_at(3), z_at(5)])
    receive(3)
    prepare(0, z_at(4))
    ff_in([z_at(4)])
    gathers[3](4)
    gathers[3](5)

    def rows_of(h):
        return pl.ds(h * QTR, QTR)

    def partial(zd, h):
        xw, yw = w_index(zd)
        rhs = jnp.concatenate(
            [
                jnp.concatenate([W[xw, yw + e, cc, D_AT + b] for e in range(2)], axis=1)
                for cc in range(2)
                for b in range(4)
            ],
            axis=0,
        )
        return jnp.dot(H[rows_of(h), :], rhs, preferred_element_type=F32)

    copies = {}
    for d in (0, 1):
        RB2[d] = partial(z_at(4), d).astype(BF16)
        copies[d, 0, d] = ring_copy(40, RB2.at[d], RS2.at[d, 0, d], d, 0, d)
        go(copies[d, 0, d])
    for s in (1, 2, 3):
        for d, h in ((0, 1), (1, 0), (0, 0), (1, 1)):
            part = partial(z_at(4 - s) if d == 0 else z_at(4 + s), h)
            slot = RS2.at[d, s - 1, h]
            if (d, s - 1, h) in copies:
                copies[d, s - 1, h].wait_recv()
                part = part + slot[...].astype(F32)
            slot[...] = part.astype(BF16)
            copies[d, s, h] = ring_copy(40, slot, RS2.at[d, s, h], d, s, h)
            go(copies[d, s, h])
    mine = pl.ds(pl.multiple_of(z * 256, 256), 256)
    for h in (1, 0):
        total = partial(z, h)
        copies[0, 3, h].wait_recv()
        copies[1, 3, h].wait_recv()
        total = total + RS2[0, 3, h].astype(F32) + RS2[1, 3, h].astype(F32)
        carried = jnp.concatenate([AGB[4 * h + i, :, mine] for i in range(4)], axis=0)
        fin = (carried.astype(F32) + total).astype(BF16)
        FIN[c, rows_of(h), :] = jnp.where(c == 0, fin[:, :B], fin[:, B:])
        FSND[rows_of(h), :] = jnp.where(c == 0, fin[:, B:], fin[:, :B])
    swap = remote(FSND, FIN.at[c], dsend.at[0], drecv.at[0], dev_c)
    go(swap)

    def put_own(t, _):
        rows = pl.ds(pl.multiple_of(t * 256, 256), 256)
        P1[rows, :] = jnp.dot(
            XN[rows, pl.ds(pl.multiple_of(c * HALF, B), HALF)], FIN[c], preferred_element_type=F32
        ).astype(BF16)
        return 0

    lax.fori_loop(0, 8, put_own, 0)
    swap.wait_recv()
    cols = pl.ds(pl.multiple_of((2 * z + c) * B, B), B)

    def put(t, _):
        rows = pl.ds(pl.multiple_of(t * 256, 256), 256)
        part = jnp.dot(
            XN[rows, pl.ds(pl.multiple_of((1 - c) * HALF, B), HALF)], FIN[1 - c],
            preferred_element_type=F32,
        )
        value = part + P1[rows, :].astype(F32)
        old = X[rows, cols].astype(F32)
        out_ref[rows, :] = jnp.where(LIVE[rows, :].astype(F32) > 0.5, value, old).astype(BF16)
        return 0

    lax.fori_loop(0, 8, put, 0)
    for cp in sent:
        cp.wait_send()


def body(
    tokens, segment_ids, row_order, row_counts, first_gain, second_gain,
    query_weight, key_weight, value_weight, output_weight, gate_weight, up_weight, down_weight,
):
    vm = pl.BlockSpec(memory_space=pltpu.VMEM)
    anyspace = pl.BlockSpec(memory_space=pl.ANY)
    smem = pl.BlockSpec(memory_space=pltpu.SMEM)
    return pl.pallas_call(
        kernel,
        out_shape=jax.ShapeDtypeStruct((ROWS, B), BF16),
        in_specs=[anyspace, vm, vm, smem, vm, vm] + [anyspace] * 7,
        out_specs=vm,
        scratch_shapes=[
            pltpu.VMEM((NX, NY, 2, BLOCKS, B, B), BF16),
            pltpu.VMEM((ROWS, D), BF16),
            pltpu.VMEM((ROWS, D), BF16),
            pltpu.VMEM((ROWS, B), BF16),
            pltpu.VMEM((ROWS, B), BF16),
            pltpu.VMEM((ROWS, B), BF16),
            pltpu.VMEM((ROWS, B), BF16),
            pltpu.VMEM((2 * HALF, ROWS), BF16),
            pltpu.VMEM((2 * HALF, B), BF16),
            pltpu.VMEM((16, PIECE, B), BF16),
            pltpu.VMEM((NZ, PIECE, D), BF16),
            pltpu.VMEM((3 * PIECE, D), BF16),
            pltpu.VMEM((HALF, 1024), BF16),
            pltpu.VMEM((2, 4, 2, QTR, 2 * B), BF16),
            pltpu.VMEM((2, QTR, 2 * B), BF16),
            pltpu.VMEM((2, HALF, B), BF16),
            pltpu.VMEM((HALF, B), BF16),
            pltpu.VMEM((ROWS, B), BF16),
            pltpu.VMEM((ROWS, B), BF16),
            pltpu.VMEM((NBLK, B), F32),
            pltpu.VMEM((NBLK, B), F32),
            pltpu.VMEM((NBLK, B), F32),
            pltpu.SemaphoreType.DMA((24,)),
            pltpu.SemaphoreType.DMA((4 * PER_GROUP,)),
            pltpu.SemaphoreType.DMA((4 * PER_GROUP,)),
            pltpu.SemaphoreType.DMA((56,)),
            pltpu.SemaphoreType.DMA((56,)),
            pltpu.SemaphoreType.DMA((1,)),
            pltpu.SemaphoreType.DMA((1,)),
        ],
        compiler_params=pltpu.CompilerParams(
            collective_id=0, has_side_effects=True, vmem_limit_bytes=67 * 1000 * 1000
        ),
        name="recursion_step",
    )(
        tokens,
        segment_ids.reshape(NBLK, B),
        row_order.reshape(NBLK, B),
        row_counts,
        first_gain.reshape(NBLK, B),
        second_gain.reshape(NBLK, B),
        query_weight, key_weight, value_weight, output_weight,
        gate_weight, up_weight, down_weight,
    )


def solution(mesh):
    weight = P("fsdp", ("dp", "tensor"))
    weight_t = P(("dp", "tensor"), "fsdp")
    in_specs = (
        P("fsdp", None), P("fsdp"), P("fsdp"), P(), P(), P(),
        weight, weight, weight, weight_t, weight, weight, weight_t,
    )
    return jax.shard_map(
        body, mesh=mesh, in_specs=in_specs, out_specs=weight, check_vma=False
    )
```

time: 151 us -> 133 us (0.88)
  Pallas kernels: 149 us -> 131 us
    pallas_call x1, Pallas kernels: 149 us -> 131 us  [body(): pl.pallas_call(kernel, out_shape=jax.ShapeDtypeStruct((ROWS, B), BF16), i...]
where the time goes in v2:
time: 133 us
  Pallas kernels  131 us (98%)
  local copies, waits for them, and re-layouts  1.87 us (1%)
    pallas_call x1, Pallas kernels, body(): pl.pallas_call(kernel, out_shape=jax.ShapeDtypeStruct((ROWS, B), BF16), i...  131 us

profile of v2, /device:TPU:1, one launch (start us, length us, event | category | flops | bytes accessed | tf_op | source)
XLA Modules:
  0.0 133.1 jit_solution(4480763558839349400)
XLA Ops:
  0.0 131.2 %recursion_step.1 = bf16[2048,128]{1,0:T(8,128)(2,1)} custom-call(bf16[2048,2048]{1,0:T(8,128)(2,1)} %tok_hbm.1, s32[16,128]{1,0:T(8,128)} %bitcast.4, s32[16,128]{1,0:T(8,128)} %bitcast.5, s32[16]{0:T(128)} %cnt_ref.1, f32[16,128]{1,0:T(8,128)} %bitcast.6, f32[16,128]{1,0:T(8,128)} %bitcast.7, bf16[128,128]{1,0:T(8,128)(2,1)} %wq.1, bf16[128,128]{1,0:T(8,128)(2,1)} %wk.1, ...), custom_call_target="tpu_custom_call" | custom-call | tf_op jit(solution)/shard_map/recursion_step/pallas_call | solution.py:519
  131.2 1.9 %copy.15 = bf16[2048,128]{1,0:T(8,128)(2,1)} copy(bf16[2048,128]{1,0:T(8,128)(2,1)} %recursion_step.1) | data formatting | bytes 1048576

commit v3 on v2

v3 whole, which is shorter than its diff:
```python
import math

import jax
import jax.numpy as jnp
from jax import lax
from jax.experimental import pallas as pl
from jax.experimental.pallas import tpu as pltpu
from jax.sharding import PartitionSpec as P

F32 = jnp.float32
BF16 = jnp.bfloat16
NZ = 8
NX = 4
NY = 4
B = 128
ROWS = 2048
D = 2048
HALF = 640
QTR = 320
NBLK = 16
PIECE = 80
O_AT, G_AT, U_AT, D_AT, BLOCKS = 3, 11, 15, 19, 23
SENDS = 96
SLOT = {0: 0, 1: 1, -1: 2, 2: 3, -2: 4, 3: 5, -3: 6, 4: 7, -4: 7}
STEP_OF_SLOT = (0, 1, 7, 2, 6, 3, 5, 4)


def column_of(row):
    return jnp.transpose(jnp.broadcast_to(row, (B, B)))


def kernel(
    tok_hbm, seg_ref, ord_ref, cnt_ref, g1_ref, g2_ref,
    wq, wk, wv, wo, wg, wu, wd,
    out_ref,
    W, X, XN, q, k, v, att, OHP, PICK, A2, AGB, NRM, H, RS2, RB2, FIN, FSND, P1, LIVE, OUT,
    segf, ordf, ordm,
    lsem, ssem, wrecv, z_recv,
):
    z = lax.axis_index("dp")
    j = lax.axis_index("fsdp")
    c = lax.axis_index("tensor")
    x = j // NY
    y = lax.rem(j, NY)
    xp = lax.rem(x + 1, NX)
    xm = lax.rem(x + 3, NX)
    x2 = lax.rem(x + 2, NX)
    yp = lax.rem(y + 1, NY)
    ym = lax.rem(y + 3, NY)
    y2 = lax.rem(y + 2, NY)
    dev_xp = {"fsdp": xp * NY + y}
    dev_xm = {"fsdp": xm * NY + y}
    dev_yp = {"fsdp": x * NY + yp}
    dev_ym = {"fsdp": x * NY + ym}
    dev_c = {"tensor": 1 - c}

    def z_at(step):
        return lax.rem(z + step, NZ)

    def dev_z(step, other=0):
        if other:
            return {"dp": z_at(step), "tensor": 1 - c}
        return {"dp": z_at(step)}

    barrier = pltpu.get_barrier_semaphore()
    peers = [dev_xp, dev_xm, dev_yp, dev_ym, dev_c]
    peers += [dev_z(dz, other) for dz in range(1, NZ) for other in (0, 1)]
    for dev in peers:
        pl.semaphore_signal(barrier, inc=1, device_id=dev, device_id_type=pl.DeviceIdType.MESH)

    own = W.at[x, y, c]
    spots = [(wq, 0), (wk, 1), (wv, 2), (wo, O_AT)]
    spots += [(wg.at[:, pl.ds(i * B, B)], G_AT + i) for i in range(4)]
    spots += [(wu.at[:, pl.ds(i * B, B)], U_AT + i) for i in range(4)]
    spots += [(wd.at[pl.ds(i * B, B), :], D_AT + i) for i in range(4)]
    of_local = [0] * 3 + [1] + [2] * 4 + [3] * 4 + [4] * 4
    local = [
        pltpu.make_async_copy(ref, own.at[b], lsem.at[of_local[i]])
        for i, (ref, b) in enumerate(spots)
    ]
    for i in range(4):
        local[i].start()
    tok = [
        pltpu.make_async_copy(
            tok_hbm.at[pl.ds(i * 256, 256), :], X.at[pl.ds(i * 256, 256), :], lsem.at[5 + i]
        )
        for i in range(8)
    ]
    for i in range(8):
        tok[i].start()
    for i in range(4, 16):
        local[i].start()

    pl.semaphore_wait(barrier, len(peers))

    sent, free = [], list(range(SENDS))

    class Remote:
        def __init__(self, src, dst, rs, dev):
            self.parts = src, dst, rs, dev

        def start(self):
            src, dst, rs, dev = self.parts
            self.slot = free.pop(0)
            self.copy = pltpu.make_async_remote_copy(
                src_ref=src, dst_ref=dst, send_sem=ssem.at[self.slot], recv_sem=rs,
                device_id=dev, device_id_type=pl.DeviceIdType.MESH,
            )
            self.copy.start()
            sent.append(self)

        def wait_recv(self):
            self.copy.wait_recv()

    remote = Remote

    def go(cp):
        cp.start()

    def arrived(ref, rs):
        pltpu.make_async_copy(ref, ref, rs).wait()

    def drain(keep):
        while len(sent) > keep:
            cp = sent.pop(0)
            cp.copy.wait_send()
            free.append(cp.slot)

    def plan(g, a, b, local_at=None, kind="whole"):
        nb = pl.ds(a, b - a)
        up, dn = pl.ds(0, 64), pl.ds(64, 64)
        full = pl.ds(0, 4)
        lo, hi = pl.ds(0, 2), pl.ds(2, 2)

        def cp(s, idx, dev):
            ref = W.at[idx]
            return remote(ref, ref, wrecv.at[g * 5 + s], dev)

        sizes = ((0, lo, 0, nb), (0, 0, 0, nb), (lo, full, 0, nb), (0, full, 0, nb))

        copies = [
            ((x, y, c, nb, up), dev_xp),
            ((x, y, c, nb, up), dev_xm),
            ((x, y, c, nb, dn), dev_yp),
            ((x, y, c, nb, dn), dev_ym),
            ((xm, y, c, nb, pl.ds(0, 32)), dev_xp),
            ((xp, y, c, nb, pl.ds(32, 32)), dev_xm),
            ((x, ym, c, nb, pl.ds(64, 32)), dev_yp),
            ((x, yp, c, nb, pl.ds(96, 32)), dev_ym),
            ((full, y, c, nb, up), dev_yp),
            ((full, y, c, nb, up), dev_ym),
            ((x, full, c, nb, dn), dev_xp),
            ((x, full, c, nb, dn), dev_xm),
            ((lo, ym, c, nb, up), dev_yp),
            ((hi, yp, c, nb, up), dev_ym),
            ((xm, lo, c, nb, dn), dev_xp),
            ((xp, hi, c, nb, dn), dev_xm),
        ]
        pass_on = [
            ((x, y, c, nb),),
            ((xm, y, c, nb, up), (xp, y, c, nb, up), (x, ym, c, nb, dn), (x, yp, c, nb, dn)),
            ((x2, y, c, nb, up), (x, y2, c, nb, dn)),
            ((full, ym, c, nb, up), (full, yp, c, nb, up), (xm, full, c, nb, dn), (xp, full, c, nb, dn)),
            ((full, y2, c, nb, up), (x2, full, c, nb, dn)),
        ]
        if kind == "second":
            pass_on[2] = ((full, y, c, nb, up), (x, full, c, nb, dn))
        if kind in ("first", "alone"):
            pass_on = [()] * 5

        def stage(s):
            if s == 5:
                arrived(W.at[full, full, 1 - c, nb], wrecv.at[g * 5 + 4])
                return
            if s == 0:
                arrived(own.at[nb], lsem.at[local_at])
            elif not (kind == "second" and s == 2):
                arrived(W.at[sizes[s - 1]], wrecv.at[g * 5 + s - 1])
            if s < 4 and not (kind == "first" and s == 2):
                for i in range(4 * s, 4 * s + 4):
                    go(cp(s, *copies[i]))
            for idx in pass_on[s]:
                go(cp(4, idx, dev_c))

        return stage

    w_q = plan(0, 0, 3, 0, "alone")
    w_a = plan(1, O_AT, O_AT + 1, 1, "first")
    w_c0 = plan(2, O_AT, O_AT + 3, None, "second")
    w_c1 = plan(3, O_AT + 3, O_AT + 5, None, "second")
    w_c2 = plan(4, O_AT + 5, O_AT + 8, None, "second")
    w_g = plan(5, G_AT, U_AT, 2)
    w_u = plan(6, U_AT, D_AT, 3)
    w_d = plan(7, D_AT, BLOCKS, 4)

    def ring_o(s):
        if s > 0:
            arrived(W.at[pl.ds(0, 4), 0, 0, pl.ds(0, 2 if s < 4 else 1)], z_recv.at[s - 1])
        for part in (0, 1):
            for d in (0, 1):
                if s < 3 or (s == 3 and part == d):
                    sign = 1 if d else -1
                    here, there = O_AT + SLOT[sign * s], O_AT + SLOT[sign * (s + 1)]
                    if part == 0:
                        src = W.at[pl.ds(0, 4), y, c, here, pl.ds(0, 64)]
                        dst = W.at[pl.ds(0, 4), y, c, there, pl.ds(0, 64)]
                    else:
                        src = W.at[x, pl.ds(0, 4), c, here, pl.ds(64, 64)]
                        dst = W.at[x, pl.ds(0, 4), c, there, pl.ds(64, 64)]
                    go(remote(src, dst, z_recv.at[s], dev_z(7 if d else 1)))

    w_q(0)
    w_a(0)
    w_g(0)

    segf[pl.ds(0, 8), :] = jnp.full((8, B), -1.0, F32)
    segf[pl.ds(4, NBLK), :] = seg_ref[...].astype(F32)
    k[pl.ds(0, 512), :] = jnp.zeros((512, B), BF16)
    v[pl.ds(0, 512), :] = jnp.zeros((512, B), BF16)
    order = ord_ref[...].astype(F32)
    ordf[...] = order
    rank = lax.broadcasted_iota(jnp.int32, (NBLK, B), 0) * B + lax.broadcasted_iota(
        jnp.int32, (NBLK, B), 1
    )
    ordm[...] = jnp.where(rank < cnt_ref[j], order, -1.0)
    gain1 = jnp.concatenate([g1_ref[pl.ds(i, 1), :] for i in range(NBLK)], axis=1)
    gain2 = jnp.concatenate([g2_ref[pl.ds(i, 1), :] for i in range(NBLK)], axis=1)

    def normed(data, gain):
        f = data.astype(F32)
        inv = lax.rsqrt(jnp.mean(f * f, axis=-1, keepdims=True) + 1e-05)
        return (f * inv * gain).astype(BF16)

    def norm_chunk(i):
        tok[i].wait()

        def body(r, _):
            rows = pl.ds(pl.multiple_of(i * 256 + r * 16, 16), 16)
            XN[rows, :] = normed(X[rows, :], gain1)
            return 0

        lax.fori_loop(0, 16, body, 0, unroll=4)

    lane = lax.broadcasted_iota(jnp.int32, (B, B), 1).astype(F32)
    sub = lax.broadcasted_iota(jnp.int32, (B, B), 0).astype(F32)

    def one_hot(t, _):
        rows = pl.ds(pl.multiple_of(t * B, B), B)
        col = column_of(ordf[pl.ds(t, 1), :])
        for u in range(NBLK):
            OHP[rows, pl.ds(u * B, B)] = jnp.where(col == lane + (B * u), 1.0, 0.0).astype(BF16)
        return 0

    norm_chunk(0)
    norm_chunk(1)
    norm_chunk(2)
    w_q(1)
    w_a(1)
    w_u(0)
    norm_chunk(3)
    norm_chunk(4)
    w_q(2)
    w_a(2)
    ring_o(0)
    w_g(1)
    w_d(0)
    norm_chunk(5)
    norm_chunk(6)
    norm_chunk(7)
    lax.fori_loop(0, 10, one_hot, 0)
    w_q(3)
    ring_o(1)
    w_u(1)
    drain(24)
    w_q(4)
    w_c0(2)
    w_d(1)
    ring_o(2)
    w_c1(2)

    def blocks(cc, b, count):
        return jnp.concatenate(
            [
                jnp.concatenate([W[i // NY, i % NY, cc, b + e] for e in range(count)], axis=1)
                for i in range(16)
            ],
            axis=0,
        )

    def qkv_product(m):
        rows = pl.ds(pl.multiple_of(m * 256, 256), 256)
        return jnp.dot(XN[rows, :], blocks(c, 0, 3), preferred_element_type=F32).astype(BF16)

    def qkv_store(m, r):
        rows = pl.ds(pl.multiple_of(m * 256, 256), 256)
        q[rows, :] = r[:, 0:B]
        rows = pl.ds(pl.multiple_of(512 + m * 256, 256), 256)
        k[rows, :] = r[:, B : 2 * B]
        v[rows, :] = r[:, 2 * B : 3 * B]

    scale = math.log2(math.e) / math.sqrt(B)
    below = lax.broadcasted_iota(jnp.int32, (256, 256), 1) <= lax.broadcasted_iota(
        jnp.int32, (256, 256), 0
    )

    def attend(i):
        qrows = pl.ds(pl.multiple_of(i * 256, 256), 256)
        krows = pl.ds(pl.multiple_of(i * 256, 256), 768)
        s = lax.dot_general(
            q[qrows, :], k[krows, :], (((1,), (1,)), ((), ())), preferred_element_type=F32
        )
        segq = jnp.concatenate(
            [column_of(segf[pl.ds(2 * i + 4 + e, 1), :]) for e in range(2)], axis=0
        )
        parts = [
            jnp.where(segq == segf[pl.ds(2 * i + t, 1), :], s[:, t * B : (t + 1) * B], -1e30)
            for t in range(6)
        ]
        s = jnp.concatenate(
            parts[:4]
            + [jnp.where(below[:, e * B : (e + 1) * B], parts[4 + e], -1e30) for e in range(2)],
            axis=1,
        )
        e = jnp.exp2((s - jnp.max(s, axis=-1, keepdims=True)) * scale)
        p = (e * (1.0 / jnp.sum(e, axis=-1, keepdims=True))).astype(BF16)
        return jnp.dot(p, v[krows, :], preferred_element_type=F32).astype(BF16)

    def att_store(i, value):
        att[pl.ds(pl.multiple_of(i * 256, 256), 256), :] = value

    def both(m, _):
        done = attend(m - 1)
        r = qkv_product(m)
        att_store(m - 1, done)
        qkv_store(m, r)
        return 0

    qkv_store(0, qkv_product(0))
    lax.fori_loop(1, 3, both, 0)
    ring_o(3)
    w_c0(3)
    lax.fori_loop(3, 5, both, 0)
    ring_o(4)
    w_c2(2)
    w_c1(3)
    lax.fori_loop(5, 8, both, 0)
    att_store(7, attend(7))
    w_c0(4)
    drain(32)

    def pick(cc):
        def tile(t, _):
            rows = pl.ds(pl.multiple_of(cc * HALF + t * QTR, 64), QTR)
            PICK[rows, :] = jnp.dot(
                OHP[rows, :], att[...], preferred_element_type=F32
            ).astype(BF16)
            return 0

        lax.fori_loop(0, 2, tile, 0)

    def piece_rows(zs, cc):
        return pl.ds(pl.multiple_of(cc * HALF + zs * PIECE, 16), PIECE)

    for other in (1, 0):
        cc = 1 - c if other else c
        pick(cc)
        for dz in (4, 3, 5, 2, 6, 1, 7, 0):
            if dz == 0 and other == 0:
                continue
            dev = dev_z(dz, other) if dz else dev_c
            go(remote(PICK.at[piece_rows(z_at(dz), cc)], A2.at[2 * z + c], z_recv.at[4], dev))
    A2[2 * z + c] = PICK[piece_rows(z, c), :]

    w_c2(3)
    w_c1(4)
    w_g(2)
    w_u(2)

    def row_tokens(n, _):
        cols = pl.ds(pl.multiple_of(n * 256, 256), 256)
        AGB[z, :, cols] = jnp.dot(
            OHP[piece_rows(z, c), :], X[:, cols], preferred_element_type=F32
        ).astype(BF16)
        return 0

    lax.fori_loop(0, 8, row_tokens, 0)
    w_c2(4)
    drain(40)

    def put_hot(t, _):
        rows = pl.ds(pl.multiple_of(t * B, B), B)
        base = (t * B).astype(F32)
        for u in range(10):
            XN[rows, pl.ds(u * B, B)] = jnp.where(
                ordm[pl.ds(u, 1), :] == sub + base, 1.0, 0.0
            ).astype(BF16)
        return 0

    ones = jnp.ones((2 * HALF, B), BF16)

    def live(t, _):
        rows = pl.ds(pl.multiple_of(t * 256, 256), 256)
        LIVE[rows, :] = jnp.dot(
            XN[rows, pl.ds(0, 2 * HALF)], ones, preferred_element_type=F32
        ).astype(BF16)
        return 0

    arrived(A2.at[pl.ds(0, 15)], z_recv.at[4])
    w_c0(5)
    w_c1(5)
    w_c2(5)

    def w_index(n):
        return n // 2, 2 * lax.rem(n, 2)

    def ring_copy(base, src, dst, d, s, h):
        n = base + (d * 4 + s) * 2 + h
        return remote(src, dst, z_recv.at[n], dev_z(1) if d == 0 else dev_z(7))

    ag = {}

    def ag_copy(d, s, h):
        if (d, s, h) not in ag:
            src = z_at(NZ - s) if d == 0 else z_at(s)
            ref = AGB.at[src, :, pl.ds(h * 1024, 1024)]
            ag[d, s, h] = ring_copy(8, ref, ref, d, s, h)
        return ag[d, s, h]

    def out_proj(n, _):
        xw, yw = w_index(n)
        cols = pl.ds(pl.multiple_of(n * 256, 256), 256)
        rhs = jnp.concatenate(
            [
                jnp.concatenate([W[xw, yw + e, cc, O_AT + slot] for e in range(2)], axis=1)
                for slot in range(8)
                for cc in range(2)
            ],
            axis=0,
        )
        lhs = jnp.concatenate(
            [A2[2 * z_at(STEP_OF_SLOT[slot]) + cc] for slot in range(8) for cc in range(2)], axis=1
        )
        total = jnp.dot(lhs, rhs, preferred_element_type=F32)
        AGB[z, :, cols] = (AGB[z, :, cols].astype(F32) + total).astype(BF16)
        return 0

    for h in (0, 1):
        lax.fori_loop(4 * h, 4 * h + 4, out_proj, 0)
        for d in (0, 1):
            go(ag_copy(d, 0, h))

    batches = ([z, z_at(1), z_at(7), z_at(2)], [z_at(6), z_at(3), z_at(5)], [z_at(4)])

    def prepare(at):
        zs = sum(batches, [])[at]
        for r in range(0, PIECE, 16):
            NRM[pl.ds(at * PIECE + r, 16), :] = normed(AGB[zs, pl.ds(r, 16), :], gain2)

    def ff_in(batch, begin=0, end=4):
        def body(n, _):
            cc = n // 2
            e = 2 * lax.rem(n, 2)
            lhs = NRM[pl.ds((0, 4, 7)[batch] * PIECE, len(batches[batch]) * PIECE), :]
            g = jnp.dot(lhs, blocks(cc, G_AT + e, 2), preferred_element_type=F32)
            u = jnp.dot(lhs, blocks(cc, U_AT + e, 2), preferred_element_type=F32)
            hid = (g / (1.0 + jnp.exp(-g)) * u).astype(BF16)
            cols = pl.ds(pl.multiple_of(n * 256, 256), 256)
            for i, zs in enumerate(batches[batch]):
                H[pl.ds(pl.multiple_of(zs * PIECE, 16), PIECE), cols] = hid[
                    i * PIECE : (i + 1) * PIECE
                ]
            return 0

        lax.fori_loop(begin, end, body, 0)

    def receive(s, h):
        for d in (0, 1):
            if s == 3 and h != d:
                continue
            ag_copy(d, s, h).wait_recv()
            if s < 2 or (s == 2 and h == d):
                go(ag_copy(d, s + 1, h))

    prepare(0)
    lax.fori_loop(0, 16, put_hot, 0)
    w_g(3)
    w_d(2)
    lax.fori_loop(0, 8, live, 0)
    receive(0, 0)
    drain(40)
    receive(0, 1)
    w_u(3)
    prepare(1)
    prepare(2)
    drain(40)
    receive(1, 0)
    w_g(4)
    receive(1, 1)
    w_d(3)
    prepare(3)
    prepare(4)
    drain(40)
    receive(2, 0)
    w_u(4)
    w_g(5)
    w_u(5)
    ff_in(0, 0, 2)
    receive(2, 1)
    w_d(4)
    ff_in(0, 2, 4)
    prepare(5)
    prepare(6)
    ff_in(1)
    receive(3, 0)
    receive(3, 1)
    prepare(7)
    ff_in(2)
    w_d(5)

    def rows_of(h):
        return pl.ds(h * QTR, QTR)

    def partial(zd, h):
        xw, yw = w_index(zd)
        rhs = jnp.concatenate(
            [
                jnp.concatenate([W[xw, yw + e, cc, D_AT + b] for e in range(2)], axis=1)
                for cc in range(2)
                for b in range(4)
            ],
            axis=0,
        )
        return jnp.dot(H[rows_of(h), :], rhs, preferred_element_type=F32)

    copies = {}
    for d in (0, 1):
        RB2[d] = partial(z_at(4), d).astype(BF16)
        copies[d, 0, d] = ring_copy(24, RB2.at[d], RS2.at[d, 0, d], d, 0, d)
        go(copies[d, 0, d])
    for s in (1, 2, 3):
        for d, h in ((0, 1), (1, 0), (0, 0), (1, 1)):
            part = partial(z_at(4 - s) if d == 0 else z_at(4 + s), h)
            slot = RS2.at[d, s - 1, h]
            if (d, s - 1, h) in copies:
                copies[d, s - 1, h].wait_recv()
                part = part + slot[...].astype(F32)
            slot[...] = part.astype(BF16)
            copies[d, s, h] = ring_copy(24, slot, RS2.at[d, s, h], d, s, h)
            go(copies[d, s, h])
        drain(16)
    mine = pl.ds(pl.multiple_of(z * 256, 256), 256)
    for h in (1, 0):
        total = partial(z, h)
        copies[0, 3, h].wait_recv()
        copies[1, 3, h].wait_recv()
        total = total + RS2[0, 3, h].astype(F32) + RS2[1, 3, h].astype(F32)
        carried = jnp.concatenate([AGB[4 * h + i, :, mine] for i in range(4)], axis=0)
        fin = (carried.astype(F32) + total).astype(BF16)
        FIN[c, rows_of(h), :] = jnp.where(c == 0, fin[:, :B], fin[:, B:])
        FSND[rows_of(h), :] = jnp.where(c == 0, fin[:, B:], fin[:, :B])
    swap = remote(FSND, FIN.at[c], z_recv.at[5], dev_c)
    go(swap)

    def put_own(t, _):
        rows = pl.ds(pl.multiple_of(t * 256, 256), 256)
        P1[rows, :] = jnp.dot(
            XN[rows, pl.ds(pl.multiple_of(c * HALF, B), HALF)], FIN[c], preferred_element_type=F32
        ).astype(BF16)
        return 0

    lax.fori_loop(0, 8, put_own, 0)
    swap.wait_recv()
    cols = pl.ds(pl.multiple_of((2 * z + c) * B, B), B)

    def put(t, _):
        rows = pl.ds(pl.multiple_of(t * 256, 256), 256)
        part = jnp.dot(
            XN[rows, pl.ds(pl.multiple_of((1 - c) * HALF, B), HALF)], FIN[1 - c],
            preferred_element_type=F32,
        )
        value = part + P1[rows, :].astype(F32)
        old = X[rows, cols].astype(F32)
        OUT[rows, :] = jnp.where(LIVE[rows, :].astype(F32) > 0.5, value, old).astype(BF16)
        store(t).start()
        return 0

    def store(t):
        rows = pl.ds(pl.multiple_of(t * 256, 256), 256)
        return pltpu.make_async_copy(OUT.at[rows, :], out_ref.at[rows, :], lsem.at[5 + t])

    lax.fori_loop(0, 8, put, 0)
    for t in range(8):
        store(t).wait()
    drain(0)


def body(
    tokens, segment_ids, row_order, row_counts, first_gain, second_gain,
    query_weight, key_weight, value_weight, output_weight, gate_weight, up_weight, down_weight,
):
    vm = pl.BlockSpec(memory_space=pltpu.VMEM)
    anyspace = pl.BlockSpec(memory_space=pl.ANY)
    smem = pl.BlockSpec(memory_space=pltpu.SMEM)
    return pl.pallas_call(
        kernel,
        out_shape=jax.ShapeDtypeStruct((ROWS, B), BF16),
        in_specs=[anyspace, vm, vm, smem, vm, vm] + [anyspace] * 7,
        out_specs=anyspace,
        scratch_shapes=[
            pltpu.VMEM((NX, NY, 2, BLOCKS, B, B), BF16),
            pltpu.VMEM((ROWS, D), BF16),
            pltpu.VMEM((ROWS, D), BF16),
            pltpu.VMEM((ROWS, B), BF16),
            pltpu.VMEM((ROWS + 512, B), BF16),
            pltpu.VMEM((ROWS + 512, B), BF16),
            pltpu.VMEM((ROWS, B), BF16),
            pltpu.VMEM((2 * HALF, ROWS), BF16),
            pltpu.VMEM((2 * HALF, B), BF16),
            pltpu.VMEM((16, PIECE, B), BF16),
            pltpu.VMEM((NZ, PIECE, D), BF16),
            pltpu.VMEM((HALF, D), BF16),
            pltpu.VMEM((HALF, 1024), BF16),
            pltpu.VMEM((2, 4, 2, QTR, 2 * B), BF16),
            pltpu.VMEM((2, QTR, 2 * B), BF16),
            pltpu.VMEM((2, HALF, B), BF16),
            pltpu.VMEM((HALF, B), BF16),
            pltpu.VMEM((ROWS, B), BF16),
            pltpu.VMEM((ROWS, B), BF16),
            pltpu.VMEM((ROWS, B), BF16),
            pltpu.VMEM((24, B), F32),
            pltpu.VMEM((NBLK, B), F32),
            pltpu.VMEM((NBLK, B), F32),
            pltpu.SemaphoreType.DMA((13,)),
            pltpu.SemaphoreType.DMA((SENDS,)),
            pltpu.SemaphoreType.DMA((8 * 5,)),
            pltpu.SemaphoreType.DMA((40,)),
        ],
        compiler_params=pltpu.CompilerParams(
            collective_id=0, has_side_effects=True, vmem_limit_bytes=67 * 1000 * 1000
        ),
        name="recursion_step",
    )(
        tokens,
        segment_ids.reshape(NBLK, B),
        row_order.reshape(NBLK, B),
        row_counts,
        first_gain.reshape(NBLK, B),
        second_gain.reshape(NBLK, B),
        query_weight, key_weight, value_weight, output_weight,
        gate_weight, up_weight, down_weight,
    )


def solution(mesh):
    weight = P("fsdp", ("dp", "tensor"))
    weight_t = P(("dp", "tensor"), "fsdp")
    in_specs = (
        P("fsdp", None), P("fsdp"), P("fsdp"), P(), P(), P(),
        weight, weight, weight, weight_t, weight, weight, weight_t,
    )
    return jax.shard_map(
        body, mesh=mesh, in_specs=in_specs, out_specs=weight, check_vma=False
    )
```

time: 133 us -> 122 us (0.917)
  Pallas kernels: 131 us -> 120 us
    pallas_call x1, Pallas kernels: 131 us -> 120 us  [body(): pl.pallas_call(kernel, out_shape=jax.ShapeDtypeStruct((ROWS, B), BF16), i...]
where the time goes in v3:
time: 122 us
  Pallas kernels  120 us (98%)
  local copies, waits for them, and re-layouts  1.87 us (2%)
    pallas_call x1, Pallas kernels, body(): pl.pallas_call(kernel, out_shape=jax.ShapeDtypeStruct((ROWS, B), BF16), i...  120 us

profile of v3, /device:TPU:1, one launch (start us, length us, event | category | flops | bytes accessed | tf_op | source)
XLA Modules:
  0.0 122.2 jit_solution(13603106425150154109)
XLA Ops:
  0.0 120.3 %recursion_step.1 = bf16[2048,128]{1,0:T(8,128)(2,1)} custom-call(bf16[2048,2048]{1,0:T(8,128)(2,1)} %tok_hbm.1, s32[16,128]{1,0:T(8,128)} %bitcast.4, s32[16,128]{1,0:T(8,128)} %bitcast.5, s32[16]{0:T(128)} %cnt_ref.1, f32[16,128]{1,0:T(8,128)} %bitcast.6, f32[16,128]{1,0:T(8,128)} %bitcast.7, bf16[128,128]{1,0:T(8,128)(2,1)} %wq.1, bf16[128,128]{1,0:T(8,128)(2,1)} %wk.1, ...), custom_call_target="tpu_custom_call" | custom-call | tf_op jit(solution)/shard_map/recursion_step/pallas_call | solution.py:604
  120.3 1.9 %copy.15 = bf16[2048,128]{1,0:T(8,128)(2,1)} copy(bf16[2048,128]{1,0:T(8,128)(2,1)} %recursion_step.1) | data formatting | bytes 1048576

commit v4 on v3

--- a/solution.py
+++ b/solution.py
@@ -30,11 +30,11 @@
 
 
 def kernel(
-    tok_hbm, seg_ref, ord_ref, cnt_ref, g1_ref, g2_ref,
+    tok_hbm, seg_hbm, ord_hbm, cnt_ref, g1_hbm, g2_hbm,
     wq, wk, wv, wo, wg, wu, wd,
     out_ref,
     W, X, XN, q, k, v, att, OHP, PICK, A2, AGB, NRM, H, RS2, RB2, FIN, FSND, P1, LIVE, OUT,
-    segf, ordf, ordm,
+    segf, ordf, ordm, seg_ref, ord_ref, g1_ref, g2_ref,
     lsem, ssem, wrecv, z_recv,
 ):
     z = lax.axis_index("dp")
@@ -86,6 +86,14 @@
         )
         for i in range(8)
     ]
+    small = [
+        pltpu.make_async_copy(src, dst, lsem.at[13 + i])
+        for i, (src, dst) in enumerate(
+            ((seg_hbm, seg_ref), (ord_hbm, ord_ref), (g1_hbm, g1_ref), (g2_hbm, g2_ref))
+        )
+    ]
+    for cp in small:
+        cp.start()
     for i in range(8):
         tok[i].start()
     for i in range(4, 16):
@@ -99,15 +107,18 @@
         def __init__(self, src, dst, rs, dev):
             self.parts = src, dst, rs, dev
 
-        def start(self):
+        def make(self):
             src, dst, rs, dev = self.parts
             self.slot = free.pop(0)
             self.copy = pltpu.make_async_remote_copy(
                 src_ref=src, dst_ref=dst, send_sem=ssem.at[self.slot], recv_sem=rs,
                 device_id=dev, device_id_type=pl.DeviceIdType.MESH,
             )
+            sent.append(self)
+
+        def start(self):
+            self.make()
             self.copy.start()
-            sent.append(self)
 
         def wait_recv(self):
             self.copy.wait_recv()
@@ -116,6 +127,15 @@
 
     def go(cp):
         cp.start()
+
+    def go_on_even(cp):
+        cp.make()
+
+        @pl.when(c == 0)
+        def _():
+            cp.copy.start()
+
+        return cp.copy
 
     def arrived(ref, rs):
         pltpu.make_async_copy(ref, ref, rs).wait()
@@ -126,6 +146,13 @@
             cp.copy.wait_send()
             free.append(cp.slot)
 
+    used = []
+
+    def recv_sem(g, s):
+        if (g, s) not in used:
+            used.append((g, s))
+        return wrecv.at[used.index((g, s))]
+
     def plan(g, a, b, local_at=None, kind="whole"):
         nb = pl.ds(a, b - a)
         up, dn = pl.ds(0, 64), pl.ds(64, 64)
@@ -134,7 +161,7 @@
 
         def cp(s, idx, dev):
             ref = W.at[idx]
-            return remote(ref, ref, wrecv.at[g * 5 + s], dev)
+            return remote(ref, ref, recv_sem(g, s), dev)
 
         sizes = ((0, lo, 0, nb), (0, 0, 0, nb), (lo, full, 0, nb), (0, full, 0, nb))
 
@@ -168,17 +195,28 @@
         if kind in ("first", "alone"):
             pass_on = [()] * 5
 
-        def stage(s):
+        held = []
+
+        def stage(s, core=None):
+            if core == 1:
+                @pl.when(c == 1)
+                def _():
+                    for h in held:
+                        h.start()
+                return
             if s == 5:
-                arrived(W.at[full, full, 1 - c, nb], wrecv.at[g * 5 + 4])
+                arrived(W.at[full, full, 1 - c, nb], recv_sem(g, 4))
                 return
             if s == 0:
                 arrived(own.at[nb], lsem.at[local_at])
             elif not (kind == "second" and s == 2):
-                arrived(W.at[sizes[s - 1]], wrecv.at[g * 5 + s - 1])
+                arrived(W.at[sizes[s - 1]], recv_sem(g, s - 1))
             if s < 4 and not (kind == "first" and s == 2):
                 for i in range(4 * s, 4 * s + 4):
-                    go(cp(s, *copies[i]))
+                    if core == 0:
+                        held.append(go_on_even(cp(s, *copies[i])))
+                    else:
+                        go(cp(s, *copies[i]))
             for idx in pass_on[s]:
                 go(cp(4, idx, dev_c))
 
@@ -213,6 +251,8 @@
     w_a(0)
     w_g(0)
 
+    for cp in small:
+        cp.wait()
     segf[pl.ds(0, 8), :] = jnp.full((8, B), -1.0, F32)
     segf[pl.ds(4, NBLK), :] = seg_ref[...].astype(F32)
     k[pl.ds(0, 512), :] = jnp.zeros((512, B), BF16)
@@ -268,14 +308,14 @@
     norm_chunk(6)
     norm_chunk(7)
     lax.fori_loop(0, 10, one_hot, 0)
+    ring_o(1)
     w_q(3)
-    ring_o(1)
     w_u(1)
     drain(24)
+    ring_o(2)
     w_q(4)
     w_c0(2)
     w_d(1)
-    ring_o(2)
     w_c1(2)
 
     def blocks(cc, b, count):
@@ -303,12 +343,15 @@
         jnp.int32, (256, 256), 0
     )
 
-    def attend(i):
+    def scores(i):
         qrows = pl.ds(pl.multiple_of(i * 256, 256), 256)
         krows = pl.ds(pl.multiple_of(i * 256, 256), 768)
-        s = lax.dot_general(
+        return lax.dot_general(
             q[qrows, :], k[krows, :], (((1,), (1,)), ((), ())), preferred_element_type=F32
         )
+
+    def attend(i, s):
+        krows = pl.ds(pl.multiple_of(i * 256, 256), 768)
         segq = jnp.concatenate(
             [column_of(segf[pl.ds(2 * i + 4 + e, 1), :]) for e in range(2)], axis=0
         )
@@ -329,23 +372,23 @@
         att[pl.ds(pl.multiple_of(i * 256, 256), 256), :] = value
 
     def both(m, _):
-        done = attend(m - 1)
+        raw = scores(m - 1)
         r = qkv_product(m)
+        done = attend(m - 1, raw)
         att_store(m - 1, done)
         qkv_store(m, r)
         return 0
 
     qkv_store(0, qkv_product(0))
-    lax.fori_loop(1, 3, both, 0)
+    lax.fori_loop(1, 4, both, 0)
     ring_o(3)
+    lax.fori_loop(4, 7, both, 0)
     w_c0(3)
-    lax.fori_loop(3, 5, both, 0)
     ring_o(4)
     w_c2(2)
     w_c1(3)
-    lax.fori_loop(5, 8, both, 0)
-    att_store(7, attend(7))
-    w_c0(4)
+    lax.fori_loop(7, 8, both, 0)
+    att_store(7, attend(7, scores(7)))
     drain(32)
 
     def pick(cc):
@@ -372,9 +415,10 @@
     A2[2 * z + c] = PICK[piece_rows(z, c), :]
 
     w_c2(3)
+    w_c0(4)
     w_c1(4)
-    w_g(2)
-    w_u(2)
+    w_g(2, 0)
+    w_u(2, 0)
 
     def row_tokens(n, _):
         cols = pl.ds(pl.multiple_of(n * 256, 256), 256)
@@ -385,7 +429,6 @@
 
     lax.fori_loop(0, 8, row_tokens, 0)
     w_c2(4)
-    drain(40)
 
     def put_hot(t, _):
         rows = pl.ds(pl.multiple_of(t * B, B), B)
@@ -406,6 +449,8 @@
         return 0
 
     arrived(A2.at[pl.ds(0, 15)], z_recv.at[4])
+    w_g(2, 1)
+    w_u(2, 1)
     w_c0(5)
     w_c1(5)
     w_c2(5)
@@ -414,7 +459,7 @@
         return n // 2, 2 * lax.rem(n, 2)
 
     def ring_copy(base, src, dst, d, s, h):
-        n = base + (d * 4 + s) * 2 + h
+        n = base + d * 7 + ((0 if s == 0 else 2 * s - 1 + h) if base == 20 else (6 if s == 3 else 2 * s + h))
         return remote(src, dst, z_recv.at[n], dev_z(1) if d == 0 else dev_z(7))
 
     ag = {}
@@ -423,7 +468,7 @@
         if (d, s, h) not in ag:
             src = z_at(NZ - s) if d == 0 else z_at(s)
             ref = AGB.at[src, :, pl.ds(h * 1024, 1024)]
-            ag[d, s, h] = ring_copy(8, ref, ref, d, s, h)
+            ag[d, s, h] = ring_copy(6, ref, ref, d, s, h)
         return ag[d, s, h]
 
     def out_proj(n, _):
@@ -484,33 +529,33 @@
     prepare(0)
     lax.fori_loop(0, 16, put_hot, 0)
     w_g(3)
-    w_d(2)
     lax.fori_loop(0, 8, live, 0)
     receive(0, 0)
     drain(40)
+    w_u(3)
+    w_d(2)
     receive(0, 1)
-    w_u(3)
     prepare(1)
     prepare(2)
     drain(40)
     receive(1, 0)
     w_g(4)
     receive(1, 1)
-    w_d(3)
     prepare(3)
     prepare(4)
-    drain(40)
+    w_u(4)
     receive(2, 0)
-    w_u(4)
     w_g(5)
     w_u(5)
     ff_in(0, 0, 2)
     receive(2, 1)
-    w_d(4)
+    w_d(3)
     ff_in(0, 2, 4)
+    drain(40)
     prepare(5)
     prepare(6)
     ff_in(1)
+    w_d(4)
     receive(3, 0)
     receive(3, 1)
     prepare(7)
@@ -535,7 +580,7 @@
     copies = {}
     for d in (0, 1):
         RB2[d] = partial(z_at(4), d).astype(BF16)
-        copies[d, 0, d] = ring_copy(24, RB2.at[d], RS2.at[d, 0, d], d, 0, d)
+        copies[d, 0, d] = ring_copy(20, RB2.at[d], RS2.at[d, 0, d], d, 0, d)
         go(copies[d, 0, d])
     for s in (1, 2, 3):
         for d, h in ((0, 1), (1, 0), (0, 0), (1, 1)):
@@ -545,7 +590,7 @@
                 copies[d, s - 1, h].wait_recv()
                 part = part + slot[...].astype(F32)
             slot[...] = part.astype(BF16)
-            copies[d, s, h] = ring_copy(24, slot, RS2.at[d, s, h], d, s, h)
+            copies[d, s, h] = ring_copy(20, slot, RS2.at[d, s, h], d, s, h)
             go(copies[d, s, h])
         drain(16)
     mine = pl.ds(pl.multiple_of(z * 256, 256), 256)
@@ -604,7 +649,7 @@
     return pl.pallas_call(
         kernel,
         out_shape=jax.ShapeDtypeStruct((ROWS, B), BF16),
-        in_specs=[anyspace, vm, vm, smem, vm, vm] + [anyspace] * 7,
+        in_specs=[anyspace] * 3 + [smem] + [anyspace] * 9,
         out_specs=anyspace,
         scratch_shapes=[
             pltpu.VMEM((NX, NY, 2, BLOCKS, B, B), BF16),
@@ -630,10 +675,14 @@
             pltpu.VMEM((24, B), F32),
             pltpu.VMEM((NBLK, B), F32),
             pltpu.VMEM((NBLK, B), F32),
-            pltpu.SemaphoreType.DMA((13,)),
+            pltpu.VMEM((NBLK, B), jnp.int32),
+            pltpu.VMEM((NBLK, B), jnp.int32),
+            pltpu.VMEM((NBLK, B), F32),
+            pltpu.VMEM((NBLK, B), F32),
+            pltpu.SemaphoreType.DMA((17,)),
             pltpu.SemaphoreType.DMA((SENDS,)),
-            pltpu.SemaphoreType.DMA((8 * 5,)),
-            pltpu.SemaphoreType.DMA((40,)),
+            pltpu.SemaphoreType.DMA((30,)),
+            pltpu.SemaphoreType.DMA((34,)),
         ],
         compiler_params=pltpu.CompilerParams(
             collective_id=0, has_side_effects=True, vmem_limit_bytes=67 * 1000 * 1000

time: 122 us -> 119 us (0.975)
  Pallas kernels: 120 us -> 117 us
    pallas_call x1, Pallas kernels: 120 us -> 117 us  [body(): pl.pallas_call(kernel, out_shape=jax.ShapeDtypeStruct((ROWS, B), BF16), i...]
where the time goes in v4:
time: 119 us
  Pallas kernels  117 us (98%)
  local copies, waits for them, and re-layouts  1.87 us (2%)
    pallas_call x1, Pallas kernels, body(): pl.pallas_call(kernel, out_shape=jax.ShapeDtypeStruct((ROWS, B), BF16), i...  117 us

profile of v4, /device:TPU:1, one launch (start us, length us, event | category | flops | bytes accessed | tf_op | source)
XLA Modules:
  0.0 119.3 jit_solution(18085733138556636068)
XLA Ops:
  0.0 117.5 %recursion_step.1 = bf16[2048,128]{1,0:T(8,128)(2,1)} custom-call(bf16[2048,2048]{1,0:T(8,128)(2,1)} %tok_hbm.1, s32[16,128]{1,0:T(8,128)} %bitcast.4, s32[16,128]{1,0:T(8,128)} %bitcast.5, s32[16]{0:T(128)} %cnt_ref.1, f32[16,128]{1,0:T(8,128)} %bitcast.6, f32[16,128]{1,0:T(8,128)} %bitcast.7, bf16[128,128]{1,0:T(8,128)(2,1)} %wq.1, bf16[128,128]{1,0:T(8,128)(2,1)} %wk.1, ...), custom_call_target="tpu_custom_call" | custom-call | tf_op jit(solution)/shard_map/recursion_step/pallas_call | solution.py:649
  117.5 1.9 %copy.15 = bf16[2048,128]{1,0:T(8,128)(2,1)} copy(bf16[2048,128]{1,0:T(8,128)(2,1)} %recursion_step.1) | data formatting | bytes 1048576

commit v5 on v4

--- a/solution.py
+++ b/solution.py
@@ -414,12 +414,6 @@
             go(remote(PICK.at[piece_rows(z_at(dz), cc)], A2.at[2 * z + c], z_recv.at[4], dev))
     A2[2 * z + c] = PICK[piece_rows(z, c), :]
 
-    w_c2(3)
-    w_c0(4)
-    w_c1(4)
-    w_g(2, 0)
-    w_u(2, 0)
-
     def row_tokens(n, _):
         cols = pl.ds(pl.multiple_of(n * 256, 256), 256)
         AGB[z, :, cols] = jnp.dot(
@@ -427,7 +421,14 @@
         ).astype(BF16)
         return 0
 
-    lax.fori_loop(0, 8, row_tokens, 0)
+    lax.fori_loop(0, 4, row_tokens, 0)
+    w_c2(3)
+    w_c0(4)
+    w_c1(4)
+    w_g(2, 0)
+    w_u(2, 0)
+
+    lax.fori_loop(4, 8, row_tokens, 0)
     w_c2(4)
 
     def put_hot(t, _):

time: 119 us -> 119 us (level)
  no operation moved by 1% of the time
where the time goes in v5:
time: 119 us
  Pallas kernels  117 us (98%)
  local copies, waits for them, and re-layouts  1.87 us (2%)
    pallas_call x1, Pallas kernels, body(): pl.pallas_call(kernel, out_shape=jax.ShapeDtypeStruct((ROWS, B), BF16), i...  117 us

profile of v5, /device:TPU:1, one launch (start us, length us, event | category | flops | bytes accessed | tf_op | source)
XLA Modules:
  0.0 119.3 jit_solution(13722587098917131100)
XLA Ops:
  0.0 117.5 %recursion_step.1 = bf16[2048,128]{1,0:T(8,128)(2,1)} custom-call(bf16[2048,2048]{1,0:T(8,128)(2,1)} %tok_hbm.1, s32[16,128]{1,0:T(8,128)} %bitcast.4, s32[16,128]{1,0:T(8,128)} %bitcast.5, s32[16]{0:T(128)} %cnt_ref.1, f32[16,128]{1,0:T(8,128)} %bitcast.6, f32[16,128]{1,0:T(8,128)} %bitcast.7, bf16[128,128]{1,0:T(8,128)(2,1)} %wq.1, bf16[128,128]{1,0:T(8,128)(2,1)} %wk.1, ...), custom_call_target="tpu_custom_call" | custom-call | tf_op jit(solution)/shard_map/recursion_step/pallas_call | solution.py:650
  117.5 1.9 %copy.15 = bf16[2048,128]{1,0:T(8,128)(2,1)} copy(bf16[2048,128]{1,0:T(8,128)(2,1)} %recursion_step.1) | data formatting | bytes 1048576
